TPU v7x, 128 devices: a whole 4x4x4 slice. The times are simulated.
128 devices in a mesh: stratum: 16 (over z, y_lo, core), replica: 8 (over x, y_hi).
Axes of the slice: x: 4, y: 4 (y_hi: 2, y_lo: 2; y = y_hi * 2 + y_lo), z: 4, core: 2. Of those that a mesh axis runs over, the one named last changes fastest.
Arguments:
- user_factors: float32 [524288, 128], P(('stratum', 'replica')), may hold values from -1.8 to 1.8
- item_factors: float32 [65536, 128], P('stratum'), may hold values from -1.8 to 1.8
- ratings: bfloat16 [2, 32768, 128, 128], P(None, ('stratum', 'replica')), may hold values from -9 to 9
- user_tile: int32 [2, 32768], P(None, ('stratum', 'replica')), may hold values from 0 to 31, as said below
- item_tile: int32 [2, 32768], P(None, ('stratum', 'replica')), may hold values from 0 to 31, as said below
- live_count: int32 [2, 128], P(None, ('stratum', 'replica')), may hold values from 64 to 256, as said below
- partner: int32 [16], replicated, may hold values from 0 to 15, as said below
Outputs:
- user_out: float32 [524288, 128], P(('stratum', 'replica'))
- item_out: float32 [65536, 128], P('stratum')
Inputs may be any that keep to these rules, and one draw needn't show every extreme that they name: partner[i] = i XOR m for one m from 8 to 15, the same for every i. `user_tile`: within one device and one sub-epoch, its 256 slots name distinct pairs of user tile and item tile. `item_tile`: paired with user_tile as stated there. `live_count`: in every sub-epoch some device has all 256 slots live.
All inputs are finite; a program needn't handle non-finite values.
Results may differ from a plain program's by a relative error of at most 0.0012.
Values sent between devices are 32-bit elements; how exact they have to be, the bound alone decides.
A program may use at most 128 MiB of HBM per device.

v0:
```python
import math

import jax
import jax.numpy as jnp
from jax import lax
from jax.sharding import PartitionSpec as P

LEARNING_RATE = 0.05
WEIGHT_DECAY = 0.05


def partner_2(block, axis, apart):
    count = lax.axis_size(axis)
    route = []
    for low in range(count):
        high = low | 1 << apart
        if high != low and high < count:
            route += [(low, high), (high, low)]
    return lax.ppermute(block, axis, route)


def local_terms(
    user_rows, block_rows, rating_slots, user_index, item_index, slot_total, block_width, turns
):
    tile_edge = rating_slots.shape[-1]
    rank_width = user_rows.shape[1]
    user_count = user_rows.shape[0] // tile_edge
    item_count = block_rows.shape[0] // tile_edge
    user_low = user_rows.astype(jnp.bfloat16).reshape(user_count, tile_edge, rank_width)
    item_low = block_rows.astype(jnp.bfloat16).reshape(item_count, tile_edge, rank_width)

    def advance(step_index, running):
        grad_user, grad_item, seen_user, seen_item = running
        first_slot = step_index * block_width
        rating_part = lax.dynamic_slice_in_dim(rating_slots, first_slot, block_width, 0)
        user_part = lax.dynamic_slice_in_dim(user_index, first_slot, block_width, 0)
        item_part = lax.dynamic_slice_in_dim(item_index, first_slot, block_width, 0)
        live_mask = (first_slot + jnp.arange(block_width, dtype=jnp.int32) < slot_total).astype(
            jnp.float32
        )
        left_tiles = jnp.take(user_low, user_part, axis=0)
        right_tiles = jnp.take(item_low, item_part, axis=0)
        predicted = jnp.einsum(
            "sik,sjk->sij", left_tiles, right_tiles, preferred_element_type=jnp.float32
        )
        residual = (rating_part.astype(jnp.float32) - predicted).astype(jnp.bfloat16)
        slot_user = jnp.einsum(
            "sij,sjk->sik", residual, right_tiles, preferred_element_type=jnp.float32
        )
        slot_item = jnp.einsum(
            "sij,sik->sjk", residual, left_tiles, preferred_element_type=jnp.float32
        )
        pick_user = (user_part[:, None] == jnp.arange(user_count, dtype=jnp.int32)[None, :]).astype(
            jnp.float32
        ) * live_mask[:, None]
        pick_item = (item_part[:, None] == jnp.arange(item_count, dtype=jnp.int32)[None, :]).astype(
            jnp.float32
        ) * live_mask[:, None]
        grad_user = grad_user + jnp.einsum(
            "sa,sik->aik", pick_user, slot_user, precision=lax.Precision.HIGHEST
        )
        grad_item = grad_item + jnp.einsum(
            "sa,sik->aik", pick_item, slot_item, precision=lax.Precision.HIGHEST
        )
        return (
            grad_user,
            grad_item,
            seen_user + jnp.sum(pick_user, axis=0),
            seen_item + jnp.sum(pick_item, axis=0),
        )

    start_state = (
        jnp.zeros((user_count, tile_edge, rank_width), jnp.float32),
        jnp.zeros((item_count, tile_edge, rank_width), jnp.float32),
        jnp.zeros((user_count,), jnp.float32),
        jnp.zeros((item_count,), jnp.float32),
    )
    return lax.fori_loop(0, turns, advance, start_state)


def exchange_block(block_rows, flip_mask):
    for level in range(lax.axis_size("stratum").bit_length() - 1):
        level_set = jnp.right_shift(flip_mask, level) % 2 == 1
        other_rows = partner_2(block_rows, "stratum", level)
        block_rows = jnp.where(level_set, other_rows, block_rows)
    return block_rows


def local(user_factors, item_factors, ratings, user_tile, item_tile, live_count, partner):
    flip_mask = partner[0]
    user_rows = user_factors
    block_rows = item_factors
    tile_edge = ratings.shape[-1]
    rank_width = user_rows.shape[1]
    slot_number = ratings.shape[1]
    block_width = math.gcd(slot_number, 64)
    keep_factor = 1.0 - LEARNING_RATE * WEIGHT_DECAY
    epochs_total = ratings.shape[0]
    for epoch_index in range(epochs_total):
        slot_total = live_count[epoch_index, 0]
        turns = slot_number // block_width
        grad_user, grad_item, seen_user, seen_item = local_terms(
            user_rows,
            block_rows,
            ratings[epoch_index],
            user_tile[epoch_index],
            item_tile[epoch_index],
            slot_total,
            block_width,
            turns,
        )
        user_scale = jnp.repeat(jnp.maximum(seen_user, 1.0), tile_edge)[:, None]
        user_rows = (
            user_rows * keep_factor + LEARNING_RATE * grad_user.reshape(-1, rank_width) / user_scale
        )
        grad_rows = grad_item.reshape(-1, rank_width)
        seen_rows = jnp.repeat(seen_item, tile_edge)
        final_epoch = epoch_index + 1 == epochs_total
        total_grad, total_seen = lax.psum((grad_rows, seen_rows), "replica")
        block_rows = (
            block_rows * keep_factor
            + LEARNING_RATE * total_grad / jnp.maximum(total_seen, 1.0)[:, None]
        )
        if not final_epoch:
            block_rows = exchange_block(block_rows, flip_mask)
    return (user_rows, block_rows)


def solution(mesh):
    return jax.shard_map(
        local,
        mesh=mesh,
        in_specs=(
            P(("stratum", "replica"), None),
            P("stratum", None),
            P(None, ("stratum", "replica"), None, None),
            P(None, ("stratum", "replica")),
            P(None, ("stratum", "replica")),
            P(None, ("stratum", "replica")),
            P(),
        ),
        out_specs=(P(("stratum", "replica"), None), P("stratum", None)),
        check_vma=False,
    )
```

profile of v0, /device:TPU:0, one launch (start us, length us, event | category | flops | bytes accessed | tf_op | source)
XLA Modules:
  0.0 673.2 jit_solution(16396236926816332897)
XLA Ops:
  7.3 12.1 %slice_bitcast_fusion.1 = (bf16[256,128,128]{2,1,0:T(8,128)(2,1)}, bf16[256,128,128]{2,1,0:T(8,128)(2,1)}) fusion(bf16[2,256,128,128]{3,2,1,0:T(8,128)(2,1)} %param.15), kind=kLoop, calls=%fused_computation.83 | loop fusion | bytes 33554432 | tf_op jit(solution)/shard_map/squeeze | solution.py:105
  22.1 131.5 %while.40 = (s32[]{:T(128)}, f32[32,128,128]{2,0,1:T(8,128)}, f32[32,128,128]{2,0,1:T(8,128)}, f32[32]{0:T(128)S(1)}, f32[32]{0:T(128)S(1)}, /*index=5*/s32[256]...) while((s32[]{:T(128)}, f32[32,128,128]{2,0,1:T(8,128)}, ...), condition=%wide.region_3.0_spmd.clone, body=%wide.region_0.4_spmd.clone.sunk | while | flops 1620073728 | bytes 92289752 | solution.py:78
  26.5 4.0 subtract_convert_fusion.4
  34.1 8.1 %select_add_fusion.9 = f32[32,128,128]{2,0,1:T(8,128)} fusion(f32[32,128,128]{2,0,1:T(8,128)} %get-tuple-element.700, f32[64,128,128]{2,1,0:T(8,128)} %fusion.78, pred[]{:T(512)S(6)} %compare.10, s32[64]{0:T(128)S(1)} %get-tuple-element.662, f32[64]{0:T(128)S(1)} %compare_convert_fusion.4), kind=kOutput, calls=%fused_computation.9.clone.1 | convolution fusion | flops 403705856 | bytes 8389121 | tf_op jit(solution)/shard_map/while/body/eval_jaxpr/sa,sik->aik/dot_general | solution.py:62
  43.9 5.6 select_add_fusion.8
  55.5 4.0 subtract_convert_fusion.4
  59.5 2.9 fusion.78
  63.1 8.8 %select_add_fusion.9 = f32[32,128,128]{2,0,1:T(8,128)} fusion(f32[32,128,128]{2,0,1:T(8,128)} %get-tuple-element.700, f32[64,128,128]{2,1,0:T(8,128)} %fusion.78, pred[]{:T(512)S(6)} %compare.10, s32[64]{0:T(128)S(1)} %get-tuple-element.662, f32[64]{0:T(128)S(1)} %compare_convert_fusion.4), kind=kOutput, calls=%fused_computation.9.clone.1 | convolution fusion | flops 403705856 | bytes 8389121 | tf_op jit(solution)/shard_map/while/body/eval_jaxpr/sa,sik->aik/dot_general | solution.py:62
  73.5 5.6 select_add_fusion.8
  85.1 4.0 subtract_convert_fusion.4
  89.1 2.9 fusion.78
  92.7 8.8 %select_add_fusion.9 = f32[32,128,128]{2,0,1:T(8,128)} fusion(f32[32,128,128]{2,0,1:T(8,128)} %get-tuple-element.700, f32[64,128,128]{2,1,0:T(8,128)} %fusion.78, pred[]{:T(512)S(6)} %compare.10, s32[64]{0:T(128)S(1)} %get-tuple-element.662, f32[64]{0:T(128)S(1)} %compare_convert_fusion.4), kind=kOutput, calls=%fused_computation.9.clone.1 | convolution fusion | flops 403705856 | bytes 8389121 | tf_op jit(solution)/shard_map/while/body/eval_jaxpr/sa,sik->aik/dot_general | solution.py:62
  103.0 5.6 select_add_fusion.8
  114.6 4.0 subtract_convert_fusion.4
  118.7 2.9 fusion.78
  122.3 8.8 %select_add_fusion.9 = f32[32,128,128]{2,0,1:T(8,128)} fusion(f32[32,128,128]{2,0,1:T(8,128)} %get-tuple-element.700, f32[64,128,128]{2,1,0:T(8,128)} %fusion.78, pred[]{:T(512)S(6)} %compare.10, s32[64]{0:T(128)S(1)} %get-tuple-element.662, f32[64]{0:T(128)S(1)} %compare_convert_fusion.4), kind=kOutput, calls=%fused_computation.9.clone.1 | convolution fusion | flops 403705856 | bytes 8389121 | tf_op jit(solution)/shard_map/while/body/eval_jaxpr/sa,sik->aik/dot_general | solution.py:62
  132.6 5.6 select_add_fusion.8
  153.6 4.1 copy.10
  157.8 42.7 %psum.29 = f32[4096]{0:T(1024)S(1)} all-reduce(f32[4096]{0:T(1024)S(1)} %broadcast_bitcast_fusion.2), channel_id=1, replica_groups=mesh['stratum'=16,'replica'=8] {'replica'}, use_global_device_ids=true, to_apply=%region_5.7 | all-reduce | flops 4096 | bytes 32768 | tf_op jit(solution)/shard_map/psum | solution.py:119
  200.6 69.8 %all-reduce.3.cloned.1.call-done = f32[4096,128]{1,0:T(8,128)} async-done(((f32[4096,128]{1,0:T(8,128)}), f32[4096,128]{1,0:T(8,128)}) %all-reduce.3.cloned.1.call-update) | async-done | bytes 2097168 | tf_op jit(solution)/shard_map/psum | solution.py:119
  274.3 3.1 collective-permute-done
  280.2 46.8 %collective-permute-done.1 = f32[4096,128]{1,0:T(8,128)} collective-permute-done((f32[4096,128]{1,0:T(8,128)S(1)}, f32[4096,128]{1,0:T(8,128)}, u32[]{:S(2)}, u32[]{:S(2)}) %collective-permute-start.1) | collective-permute-done | bytes 2097184 | tf_op jit(solution)/shard_map/ppermute | solution.py:19
  330.1 45.6 %collective-permute-done.2 = f32[4096,128]{1,0:T(8,128)} collective-permute-done((f32[4096,128]{1,0:T(8,128)}, f32[4096,128]{1,0:T(8,128)}, u32[]{:S(2)}, u32[]{:S(2)}) %collective-permute-start.2) | collective-permute-done | bytes 2097184 | tf_op jit(solution)/shard_map/ppermute | solution.py:19
  375.7 3.1 broadcast_select_fusion.18
  378.8 3.1 collective-permute-start.3
  384.8 41.7 %collective-permute-done.3 = f32[4096,128]{1,0:T(8,128)} collective-permute-done((f32[4096,128]{1,0:T(8,128)}, f32[4096,128]{1,0:T(8,128)}, u32[]{:S(2)}, u32[]{:S(2)}) %collective-permute-start.3) | collective-permute-done | bytes 2097184 | tf_op jit(solution)/shard_map/ppermute | solution.py:19
  429.4 117.9 %while.41 = (s32[]{:T(128)}, f32[32,128,128]{2,0,1:T(8,128)}, f32[32,128,128]{2,0,1:T(8,128)}, f32[32]{0:T(128)S(1)}, f32[32]{0:T(128)S(1)}, /*index=5*/s32[256]...) while((s32[]{:T(128)}, f32[32,128,128]{2,0,1:T(8,128)}, ...), condition=%wide.region_9.11_spmd.clone, body=%wide.region_6.10_spmd.clone.sunk | while | flops 1620073728 | bytes 92289752 | solution.py:78
  433.9 4.0 subtract_convert_fusion.5
  437.9 2.9 fusion.86
  441.5 8.1 %select_add_fusion.11 = f32[32,128,128]{2,0,1:T(8,128)} fusion(f32[32,128,128]{2,0,1:T(8,128)} %get-tuple-element.745, f32[64,128,128]{2,1,0:T(8,128)} %fusion.86, pred[]{:T(512)S(6)} %compare.11, s32[64]{0:T(128)S(1)} %get-tuple-element.679, f32[64]{0:T(128)S(1)} %compare_convert_fusion.5), kind=kOutput, calls=%fused_computation.48.clone.1 | convolution fusion | flops 403705856 | bytes 8389121 | tf_op jit(solution)/shard_map/while/body/eval_jaxpr/sa,sik->aik/dot_general | solution.py:62
  451.2 5.6 select_add_fusion.10
  462.8 4.0 subtract_convert_fusion.5
  466.9 2.9 fusion.86
  470.4 8.8 %select_add_fusion.11 = f32[32,128,128]{2,0,1:T(8,128)} fusion(f32[32,128,128]{2,0,1:T(8,128)} %get-tuple-element.745, f32[64,128,128]{2,1,0:T(8,128)} %fusion.86, pred[]{:T(512)S(6)} %compare.11, s32[64]{0:T(128)S(1)} %get-tuple-element.679, f32[64]{0:T(128)S(1)} %compare_convert_fusion.5), kind=kOutput, calls=%fused_computation.48.clone.1 | convolution fusion | flops 403705856 | bytes 8389121 | tf_op jit(solution)/shard_map/while/body/eval_jaxpr/sa,sik->aik/dot_general | solution.py:62
  480.8 5.6 select_add_fusion.10
  492.4 4.0 subtract_convert_fusion.5
  496.5 2.9 fusion.86
  500.0 8.8 %select_add_fusion.11 = f32[32,128,128]{2,0,1:T(8,128)} fusion(f32[32,128,128]{2,0,1:T(8,128)} %get-tuple-element.745, f32[64,128,128]{2,1,0:T(8,128)} %fusion.86, pred[]{:T(512)S(6)} %compare.11, s32[64]{0:T(128)S(1)} %get-tuple-element.679, f32[64]{0:T(128)S(1)} %compare_convert_fusion.5), kind=kOutput, calls=%fused_computation.48.clone.1 | convolution fusion | flops 403705856 | bytes 8389121 | tf_op jit(solution)/shard_map/while/body/eval_jaxpr/sa,sik->aik/dot_general | solution.py:62
  510.4 5.6 select_add_fusion.10
  522.0 4.0 subtract_convert_fusion.5
  526.1 2.9 fusion.86
  529.6 8.8 %select_add_fusion.11 = f32[32,128,128]{2,0,1:T(8,128)} fusion(f32[32,128,128]{2,0,1:T(8,128)} %get-tuple-element.745, f32[64,128,128]{2,1,0:T(8,128)} %fusion.86, pred[]{:T(512)S(6)} %compare.11, s32[64]{0:T(128)S(1)} %get-tuple-element.679, f32[64]{0:T(128)S(1)} %compare_convert_fusion.5), kind=kOutput, calls=%fused_computation.48.clone.1 | convolution fusion | flops 403705856 | bytes 8389121 | tf_op jit(solution)/shard_map/while/body/eval_jaxpr/sa,sik->aik/dot_general | solution.py:62
  540.0 5.6 select_add_fusion.10
  547.3 4.1 copy.12
  555.9 41.7 %psum.31 = f32[4096]{0:T(1024)S(1)} all-reduce(f32[4096]{0:T(1024)S(1)} %broadcast_bitcast_fusion), channel_id=1, replica_groups=mesh['stratum'=16,'replica'=8] {'replica'}, use_global_device_ids=true, to_apply=%region_11.13 | all-reduce | flops 4096 | bytes 32768 | tf_op jit(solution)/shard_map/psum | solution.py:119
  597.7 5.3 fusion.46
  603.0 59.5 %all-reduce.5.cloned.1.call-done = f32[4096,128]{1,0:T(8,128)} async-done(((f32[4096,128]{1,0:T(8,128)}), f32[4096,128]{1,0:T(8,128)}) %all-reduce.5.cloned.1.call-update) | async-done | bytes 2097168 | tf_op jit(solution)/shard_map/psum | solution.py:119
  662.4 3.5 divide_add_fusion
  (238 shorter events, 90.5 us)
Async XLA Ops:
  7.2 263.2 %all-reduce.3.cloned.1.call-start = ((), (), s32[]{:S(2)}) async-start(), calls=%async_computation | async-start | bytes 4194304 | tf_op jit(solution)/shard_map/psum | solution.py:119
  7.2 12.2 %copy-start.18 = (s32[2,256]{1,0:T(2,128)S(1)}, s32[2,256]{1,0:T(2,128)}, u32[]{:S(2)}) copy-start(s32[2,256]{1,0:T(2,128)} %param.16) | copy-start | bytes 6148
  7.3 12.2 %copy-start.19 = (s32[2,256]{1,0:T(2,128)S(1)}, s32[2,256]{1,0:T(2,128)}, u32[]{:S(2)}) copy-start(s32[2,256]{1,0:T(2,128)} %param.17) | copy-start | bytes 6148
  7.3 12.2 %copy-start.20 = (s32[2,1]{0,1:T(1,128)S(1)}, s32[2,1]{0,1:T(1,128)}, u32[]{:S(2)}) copy-start(s32[2,1]{0,1:T(1,128)} %param.18) | copy-start | bytes 28
  7.3 12.8 %copy-start.12 = (f32[4096,128]{1,0:T(8,128)S(1)}, f32[4096,128]{1,0:T(8,128)}, u32[]{:S(2)}) copy-start(f32[4096,128]{1,0:T(8,128)} %param.13) | copy-start | bytes 6291460
  19.4 1.6 copy-start.17
  26.5 4.0 copy-start
  30.6 2.9 copy-start.2
  34.1 8.1 %copy-start.3 = (bf16[64,128,128]{2,1,0:T(8,128)(2,1)S(1)}, bf16[64,128,128]{2,1,0:T(8,128)(2,1)}, u32[]{:S(2)}) copy-start(bf16[64,128,128]{2,1,0:T(8,128)(2,1)} %copy-done.2) | copy-start | bytes 6291460 | tf_op jit(solution)/shard_map/while
  42.3 1.6 copy-start.9
  55.4 4.0 copy-start
  59.5 2.9 copy-start.2
  63.1 8.8 %copy-start.3 = (bf16[64,128,128]{2,1,0:T(8,128)(2,1)S(1)}, bf16[64,128,128]{2,1,0:T(8,128)(2,1)}, u32[]{:S(2)}) copy-start(bf16[64,128,128]{2,1,0:T(8,128)(2,1)} %copy-done.2) | copy-start | bytes 6291460 | tf_op jit(solution)/shard_map/while
  71.9 1.6 copy-start.9
  85.0 4.0 copy-start
  89.1 2.9 copy-start.2
  92.6 8.8 %copy-start.3 = (bf16[64,128,128]{2,1,0:T(8,128)(2,1)S(1)}, bf16[64,128,128]{2,1,0:T(8,128)(2,1)}, u32[]{:S(2)}) copy-start(bf16[64,128,128]{2,1,0:T(8,128)(2,1)} %copy-done.2) | copy-start | bytes 6291460 | tf_op jit(solution)/shard_map/while
  101.5 1.6 copy-start.9
  114.6 4.0 copy-start
  118.7 2.9 copy-start.2
  122.2 8.8 %copy-start.3 = (bf16[64,128,128]{2,1,0:T(8,128)(2,1)S(1)}, bf16[64,128,128]{2,1,0:T(8,128)(2,1)}, u32[]{:S(2)}) copy-start(bf16[64,128,128]{2,1,0:T(8,128)(2,1)} %copy-done.2) | copy-start | bytes 6291460 | tf_op jit(solution)/shard_map/while
  131.0 1.6 copy-start.9
  157.7 504.7 %all-reduce.5.cloned.1.call-start = ((), (), s32[]{:S(2)}) async-start(), calls=%async_computation.1 | async-start | bytes 4194304 | tf_op jit(solution)/shard_map/psum | solution.py:119
  200.6 72.5 %copy-start.21 = (s32[16]{0:T(128)S(1)}, s32[16]{0:T(128)}, u32[]{:S(2)}) copy-start(s32[16]{0:T(128)} %param.19) | copy-start | bytes 196
  272.9 4.4 collective-permute-start
  279.1 47.9 %collective-permute-start.1 = (f32[4096,128]{1,0:T(8,128)S(1)}, f32[4096,128]{1,0:T(8,128)}, u32[]{:S(2)}, u32[]{:S(2)}) collective-permute-start(f32[4096,128]{1,0:T(8,128)S(1)} %broadcast_select_fusion.16), channel_id=1, source_target_pairs={{0,16},{16,0},{8,24},{24,8},{32,48},{48,32},{40,56},{56,40},{64,80... | collective-permute-start | bytes 6291464 | tf_op jit(solution)/shard_map/ppermute | solution.py:19
  328.5 47.2 %collective-permute-start.2 = (f32[4096,128]{1,0:T(8,128)}, f32[4096,128]{1,0:T(8,128)}, u32[]{:S(2)}, u32[]{:S(2)}) collective-permute-start(f32[4096,128]{1,0:T(8,128)} %broadcast_select_fusion.17), channel_id=1, source_target_pairs={{0,32},{32,0},{8,40},{40,8},{16,48},{48,16},{24,56},{56,24},{64,96... | collective-permute-start | bytes 6291464 | tf_op jit(solution)/shard_map/ppermute | solution.py:19
  330.0 52.0 %copy-start.11 = (f32[32,128,128]{2,0,1:T(8,128)S(1)}, f32[32,128,128]{2,0,1:T(8,128)}, u32[]{:S(2)}) copy-start(f32[32,128,128]{2,0,1:T(8,128)} %get-tuple-element.377) | copy-start | bytes 6291460
  378.8 47.7 %collective-permute-start.3 = (f32[4096,128]{1,0:T(8,128)}, f32[4096,128]{1,0:T(8,128)}, u32[]{:S(2)}, u32[]{:S(2)}) collective-permute-start(f32[4096,128]{1,0:T(8,128)} %broadcast_select_fusion.18), channel_id=1, source_target_pairs={{0,64},{64,0},{8,72},{72,8},{16,80},{80,16},{24,88},{88,24},{32,96... | collective-permute-start | bytes 6291464 | tf_op jit(solution)/shard_map/ppermute | solution.py:19
  382.3 1.6 copy-start.13
  433.9 4.0 copy-start.1
  437.9 2.9 copy-start.4
  441.5 8.1 %copy-start.5 = (bf16[64,128,128]{2,1,0:T(8,128)(2,1)S(1)}, bf16[64,128,128]{2,1,0:T(8,128)(2,1)}, u32[]{:S(2)}) copy-start(bf16[64,128,128]{2,1,0:T(8,128)(2,1)} %copy-done.4) | copy-start | bytes 6291460 | tf_op jit(solution)/shard_map/while
  449.6 1.6 copy-start.6
  462.8 4.0 copy-start.1
  466.9 2.9 copy-start.4
  470.4 8.8 %copy-start.5 = (bf16[64,128,128]{2,1,0:T(8,128)(2,1)S(1)}, bf16[64,128,128]{2,1,0:T(8,128)(2,1)}, u32[]{:S(2)}) copy-start(bf16[64,128,128]{2,1,0:T(8,128)(2,1)} %copy-done.4) | copy-start | bytes 6291460 | tf_op jit(solution)/shard_map/while
  479.2 1.6 copy-start.6
  492.4 4.0 copy-start.1
  496.5 2.9 copy-start.4
  500.0 8.8 %copy-start.5 = (bf16[64,128,128]{2,1,0:T(8,128)(2,1)S(1)}, bf16[64,128,128]{2,1,0:T(8,128)(2,1)}, u32[]{:S(2)}) copy-start(bf16[64,128,128]{2,1,0:T(8,128)(2,1)} %copy-done.4) | copy-start | bytes 6291460 | tf_op jit(solution)/shard_map/while
  508.8 1.6 copy-start.6
  522.0 4.0 copy-start.1
  526.1 2.9 copy-start.4
  529.6 8.8 %copy-start.5 = (bf16[64,128,128]{2,1,0:T(8,128)(2,1)S(1)}, bf16[64,128,128]{2,1,0:T(8,128)(2,1)}, u32[]{:S(2)}) copy-start(bf16[64,128,128]{2,1,0:T(8,128)(2,1)} %copy-done.4) | copy-start | bytes 6291460 | tf_op jit(solution)/shard_map/while
  538.4 1.6 copy-start.6
  551.4 1.6 copy-start.8
  553.3 44.4 %copy-start.14 = (f32[4096,128]{1,0:T(8,128)S(1)}, f32[4096,128]{1,0:T(8,128)}, u32[]{:S(2)}) copy-start(f32[4096,128]{1,0:T(8,128)} %param.13) | copy-start | bytes 6291460
  (10 other events, 13.4 us)
Sparse Core Ops, SparseCore 0:
  157.8 112.5 all-reduce.2
  551.6 110.8 all-reduce.4
where the time goes:
time: 685 us; the launch traced here: 673 us
  waiting for transfers between devices  267 us (39%)
  matrix products  176 us (26%)
  blocking collectives  84.5 us (12%)
  local copies, waits for them, and re-layouts  80.9 us (12%)
  other arithmetic  30.1 us (4%)
  loops' own time  14.9 us (2%)
  between operations  14.9 us (2%)
    ppermute x4, waiting for transfers between devices, partner_2(): return lax.ppermute(block, axis, route)  137 us
    psum x2, waiting for transfers between devices, local(): total_grad, total_seen = lax.psum((grad_rows, seen_rows), 'replica')  129 us
    psum x2, blocking collectives, local(): total_grad, total_seen = lax.psum((grad_rows, seen_rows), 'replica')  84.5 us
    dot_general x8, matrix products, advance(): jnp.einsum('sa,sik->aik', pick_item, slot_item, precision=lax.Precision.H...  69 us
    dot_general x8, matrix products, advance(): jnp.einsum('sa,sik->aik', pick_user, slot_user, precision=lax.Precision.H...  45 us
    dot_general x8, matrix products, advance(): jnp.einsum('sik,sjk->sij', left_tiles, right_tiles, preferred_element_typ...  32.2 us
    dot_general x8, matrix products, advance(): jnp.einsum('sij,sik->sjk', residual, left_tiles, preferred_element_type=j...  23.2 us
    gather x8, local copies, waits for them, and re-layouts, advance(): right_tiles = jnp.take(item_low, item_part, axis=0)  17.4 us
  transfers between devices with their start and end apart: 6, of which 6 were waited for; matrix products, arithmetic and copies ran while one was open for 2% of the time, Pallas kernels for 0%

commit v1 on v0

v1 whole, which is shorter than its diff:
```python
import functools

import jax
import jax.numpy as jnp
from jax import lax
from jax.experimental import pallas as pl
from jax.experimental.pallas import tpu as pltpu
from jax.sharding import PartitionSpec as P

LR = 0.05
KEEP = 1.0 - 0.05*0.05
NT = (((1,), (1,)), ((), ()))
NN = (((1,), (0,)), ((), ()))
f32, bf16 = jnp.float32, jnp.bfloat16

def tile_kernel(epoch, slots, shards, chunks, group,
                ut, it, live_ref, users, items, ratings,
                users_out, grads_out,
                rat, uf, vf, ub, utb, vb, du, dv, su, si, rsem, msem):
    tiles = ub.shape[0]
    per = tiles // shards
    T = ub.shape[1]
    width = slots // chunks
    loads = [pltpu.make_async_copy(ratings.at[epoch, pl.ds(c*width, width)], rat.at[pl.ds(c*width, width)], rsem.at[c]) for c in range(chunks)]
    cu = pltpu.make_async_copy(users, uf, msem.at[0])
    cv = pltpu.make_async_copy(items, vf, msem.at[1])
    cu.start(); cv.start()
    for l in loads: l.start()

    @pl.loop(0, tiles)
    def _(b):
        su[b] = 0
        si[b] = 0
        du[b] = jnp.zeros((T, T), f32)
    @pl.loop(0, shards)
    def _(s):
        dv[s] = jnp.zeros(dv.shape[1:], f32)
    eye = (lax.broadcasted_iota(jnp.int32, (T, T), 0) == lax.broadcasted_iota(jnp.int32, (T, T), 1)).astype(bf16)
    cu.wait()
    @pl.loop(0, tiles, step=4)
    def _(b0):
        for k in range(4):
            b = b0 + k
            x = uf[pl.ds(b*T, T), :].astype(bf16)
            ub[b] = x
            utb[b] = lax.dot_general(eye, x, NT, preferred_element_type=f32).astype(bf16)
    cv.wait()
    @pl.loop(0, tiles, step=4)
    def _(b0):
        for k in range(4):
            b = b0 + k
            vb[b] = vf[pl.ds(b*T, T), :].astype(bf16)
    live = live_ref[epoch, 0]

    for c in range(chunks):
        loads[c].wait()
        base = c*width
        count = jnp.clip(live - base, 0, width)
        @pl.loop(0, pl.cdiv(count, group))
        def _(j):
            t0 = base + j*group
            aa, bb, rr = [], [], []
            for k in range(group):
                t = t0 + k
                a = ut[epoch, t]; b = it[epoch, t]
                aa.append(a); bb.append(b)
            for k in range(group):
                t = t0 + k
                p = lax.dot_general(ub[aa[k]], vb[bb[k]], NT, preferred_element_type=f32)
                r = rat[t].astype(f32) - p
                if k:
                    r = jnp.where(t < live, r, 0.0)
                rr.append(r.astype(bf16))
            gu = [lax.dot_general(rr[k], vb[bb[k]], NN, preferred_element_type=f32) for k in range(group)]
            gv = [lax.dot_general(utb[aa[k]], rr[k], NN, preferred_element_type=f32) for k in range(group)]
            for k in range(group):
                one = (t0 + k < live).astype(jnp.int32)
                du[aa[k]] += gu[k]
                s = bb[k] // per
                o = pl.multiple_of((bb[k] % per)*T, T)
                dv[s, pl.ds(o, T), :] += gv[k]
                su[aa[k]] = su[aa[k]] + one
                si[bb[k]] = si[bb[k]] + one
    row = lax.broadcasted_iota(jnp.int32, (8, T), 0)
    for s in range(shards):
        z = jnp.zeros((8, T), f32)
        for k in range(per):
            z = jnp.where(row == k, si[s*per+k].astype(f32), z)
        dv[s, pl.ds(per*T, 8), :] = z
    og = pltpu.make_async_copy(dv, grads_out, msem.at[2])
    og.start()
    @pl.loop(0, tiles, step=2)
    def _(b0):
        for k in range(2):
            b = b0 + k
            cnt = jnp.full((1, T), jnp.maximum(su[b], 1), jnp.int32).astype(f32)
            sl = pl.ds(pl.multiple_of(b*T, T), T)
            uf[sl, :] = uf[sl, :]*KEEP + du[b]*(LR/cnt)
    ou = pltpu.make_async_copy(uf, users_out, msem.at[3])
    ou.start()
    og.wait(); ou.wait()

def tiles_step(epoch, ut, it, live, users, items, ratings, shards=8, chunks=8, group=16):
    slots, T = ratings.shape[1], ratings.shape[2]
    tiles = users.shape[0]//T
    per = tiles//shards
    smem = pl.BlockSpec(memory_space=pltpu.SMEM)
    anyb = pl.BlockSpec(memory_space=pl.ANY)
    return pl.pallas_call(
        functools.partial(tile_kernel, epoch, slots, shards, chunks, group),
        out_shape=(jax.ShapeDtypeStruct(users.shape, f32), jax.ShapeDtypeStruct((shards, per*T+8, T), f32)),
        in_specs=[smem]*3+[anyb]*3, out_specs=(anyb, anyb),
        scratch_shapes=[pltpu.VMEM((slots,T,T),bf16), pltpu.VMEM(users.shape,f32), pltpu.VMEM(items.shape,f32),
            pltpu.VMEM((tiles,T,T),bf16),pltpu.VMEM((tiles,T,T),bf16),pltpu.VMEM((tiles,T,T),bf16),
            pltpu.VMEM((tiles,T,T),f32), pltpu.VMEM((shards,per*T+8,T),f32),
            pltpu.SMEM((tiles,),jnp.int32),pltpu.SMEM((tiles,),jnp.int32),
            pltpu.SemaphoreType.DMA((chunks,)), pltpu.SemaphoreType.DMA((4,))],
        compiler_params=pltpu.CompilerParams(vmem_limit_bytes=48<<20),
        name="tile_step",
    )(ut, it, live, users, items, ratings)


MESH = pl.DeviceIdType.MESH

def share_kernel(mask, n, grads, block, out, mine, parts, rows, incoming, s_rs, r_rs, s_ag, r_ag, s_ex, r_ex, lsem):
    s = lax.axis_index("stratum")
    r = lax.axis_index("replica")
    T = block.shape[1]
    height = rows.shape[0]
    bar = pltpu.get_barrier_semaphore()
    for k in range(1, n):
        pl.semaphore_signal(bar, inc=1, device_id=(s, lax.rem(r + k, n)), device_id_type=MESH)
    if mask:
        across = s + 0
        for bit in range(4):
            if mask >> bit & 1:
                across = across + (1 << bit) - 2 * (1 << bit) * (lax.rem(lax.div(s, 1 << bit), 2))
        pl.semaphore_signal(bar, inc=1, device_id=(across, r), device_id_type=MESH)
    cb = pltpu.make_async_copy(block.at[pl.ds(r * height, height)], rows, lsem.at[0])
    cb.start()
    cm = pltpu.make_async_copy(grads.at[r], mine, lsem.at[1])
    cm.start()
    pl.semaphore_wait(bar, n - 1 + (1 if mask else 0))
    outs = []
    for k in range(1, n):
        q = lax.rem(r + k, n)
        c = pltpu.make_async_remote_copy(src_ref=grads.at[q], dst_ref=parts.at[k - 1], send_sem=s_rs.at[k - 1], recv_sem=r_rs.at[k - 1], device_id=(s, q), device_id_type=MESH)
        c.start()
        outs.append(c)
    cm.wait()
    cb.wait()
    for k in range(n - 1):
        outs[k].wait_recv()
        mine[...] += parts[k]
    per = height // T
    for k in range(per):
        cnt = jnp.maximum(mine[pl.ds(height + k, 1), :], 1.0)
        sl = pl.ds(k * T, T)
        rows[sl, :] = rows[sl, :] * KEEP + mine[sl, :].T * (LR / cnt)
    if mask:
        ex = pltpu.make_async_remote_copy(src_ref=rows, dst_ref=incoming, send_sem=s_ex, recv_sem=r_ex, device_id=(across, r), device_id_type=MESH)
        ex.start()
        ex.wait()
        src = incoming
    else:
        src = rows
    lc = pltpu.make_async_copy(src, out.at[pl.ds(r * height, height)], lsem.at[0])
    lc.start()
    gs = []
    for k in range(1, n):
        q = lax.rem(r + k, n)
        c = pltpu.make_async_remote_copy(src_ref=src, dst_ref=out.at[pl.ds(r * height, height)], send_sem=s_ag.at[k - 1], recv_sem=r_ag.at[k - 1], device_id=(s, q), device_id_type=MESH)
        c.start()
        gs.append(c)
    for c in outs: c.wait_send()
    lc.wait()
    for c in gs: c.wait()


def share(grads, block, mask, cid, n):
    height = block.shape[0] // n
    anyb = pl.BlockSpec(memory_space=pl.ANY)
    T = block.shape[1]
    sems = lambda k: pltpu.SemaphoreType.DMA((k,))
    return pl.pallas_call(
        functools.partial(share_kernel, mask, n),
        out_shape=jax.ShapeDtypeStruct(block.shape, f32),
        in_specs=[anyb, anyb],
        out_specs=anyb,
        scratch_shapes=[
            pltpu.VMEM(grads.shape[1:], f32),
            pltpu.VMEM((n - 1, *grads.shape[1:]), f32),
            pltpu.VMEM((height, T), f32),
            pltpu.VMEM((height, T), f32),
            sems(n - 1), sems(n - 1), sems(n - 1), sems(n - 1),
            pltpu.SemaphoreType.DMA, pltpu.SemaphoreType.DMA, sems(2),
        ],
        compiler_params=pltpu.CompilerParams(collective_id=cid, has_side_effects=True),
        name=f"share_{mask}",
    )(grads, block)


def local(user_factors, item_factors, ratings, user_tile, item_tile, live_count, partner):
    n = lax.axis_size("replica")
    half = lax.axis_size("stratum") // 2
    users, grads = tiles_step(0, user_tile, item_tile, live_count, user_factors, item_factors, ratings, n)
    branches = [functools.partial(share, mask=half + k, cid=1 + k, n=n) for k in range(half)]
    block = lax.switch(partner[0] - half, branches, grads, item_factors)
    users, grads = tiles_step(1, user_tile, item_tile, live_count, users, block, ratings, n)
    return users, share(grads, block, 0, 0, n)


def solution(mesh):
    return jax.shard_map(
        local,
        mesh=mesh,
        in_specs=(
            P(("stratum", "replica"), None),
            P("stratum", None),
            P(None, ("stratum", "replica"), None, None),
            P(None, ("stratum", "replica")),
            P(None, ("stratum", "replica")),
            P(None, ("stratum", "replica")),
            P(),
        ),
        out_specs=(P(("stratum", "replica"), None), P("stratum", None)),
        check_vma=False,
    )
```

time: 685 us -> 182 us (0.27)
  the two profiles are of different devices: /device:TPU:0 before, /device:TPU:60 now
where the time goes in v1:
time: 182 us
  Pallas kernels  172 us (95%)
  local copies, waits for them, and re-layouts  8.08 us (4%)
    pallas_call x2, Pallas kernels, share(): pl.pallas_call(functools.partial(share_kernel, mask, n), out_shape=jax.Sh...  143 us
    pallas_call x2, Pallas kernels, tiles_step(): pl.pallas_call(functools.partial(tile_kernel, epoch, slots, shards, chunk...  29.5 us
    unnamed x14, local copies, waits for them, and re-layouts  8.08 us

profile of v1, /device:TPU:60, one launch (start us, length us, event | category | flops | bytes accessed | tf_op | source)
XLA Modules:
  0.0 181.8 jit_solution(896143206352013594)
XLA Ops:
  1.3 0.7 copy.10.live_ref
  2.0 0.0 copy-start.1
  2.0 1.6 copy-done.1
  3.6 0.0 copy-start.2
  3.6 0.7 copy-done.2
  4.3 0.0 copy-start.4
  4.3 0.7 copy-done.4
  5.0 17.6 %tile_step.2 = (f32[4096,128]{1,0:T(8,128)S(1)}, f32[8,520,128]{2,1,0:T(8,128)}) custom-call(s32[2,256]{1,0:T(2,128)S(1)} %copy-done.2, s32[2,256]{1,0:T(2,128)S(1)} %copy-done.4, s32[2,1]{1,0:T(2,128)S(1)} %copy.10.live_ref, f32[4096,128]{1,0:T(8,128)S(1)} %copy-done.1, f32[4096,128]{1,0:T(8,128)} %items.1, bf16[2,256,128,128]{3,2,1,0:T(8,128)(2,1)} %ratings.3), custom_call_target="tpu_custom_call" | custom-call | tf_op jit(solution)/shard_map/tile_step/pallas_call | solution.py:109
  22.6 0.0 copy-start.3
  22.6 0.0 copy-start.5
  22.6 70.0 %conditional.1 = (f32[4096,128]{1,0:T(8,128)}) conditional(s32[]{:T(128)} %bitcast, (f32[8,520,128]{2,1,0:T(8,128)}, f32[4096,128]{1,0:T(8,128)}) %tuple.32, (f32[8,520,128]{2,1,0:T(8,128)}, f32[4096,128]{1,0:T(8,128)}) %tuple.32, (f32[8,520,128]{2,1,0:T(8,128)}, f32[4096,128]{1,0:T(8,128)}) %tuple.32, ...), branch_computations={%region_0.0_spmd, %region_1.0_spmd, %region_2.0_spmd, %region_3.0_... | conditional | bytes 8 | solution.py:208
  22.7 70.0 %share_12.1 = f32[4096,128]{1,0:T(8,128)} custom-call(f32[8,520,128]{2,1,0:T(8,128)} %get-tuple-element.49.grads, f32[4096,128]{1,0:T(8,128)} %get-tuple-element.50.block), custom_call_target="tpu_custom_call" | custom-call | tf_op jit(solution)/shard_map/cond/branch_4_fun/share_12/pallas_call | solution.py:185
  92.7 0.0 copy-done.3
  92.7 0.0 copy-done.5
  92.7 11.9 %tile_step.3 = (f32[4096,128]{1,0:T(8,128)}, f32[8,520,128]{2,1,0:T(8,128)S(1)}) custom-call(s32[2,256]{1,0:T(2,128)S(1)} %copy-done.3, s32[2,256]{1,0:T(2,128)S(1)} %copy-done.5, s32[2,1]{1,0:T(2,128)S(1)} %copy.10.live_ref, f32[4096,128]{1,0:T(8,128)S(1)} %get-tuple-element.63.users, f32[4096,128]{1,0:T(8,128)} %get-tuple-element.71.items.block, ...), custom_call_target="tpu_custom_call" | custom-call | tf_op jit(solution)/shard_map/tile_step/pallas_call | solution.py:109
  104.6 0.0 copy-start
  104.6 1.3 copy-done
  105.9 72.8 %share_0.1 = f32[4096,128]{1,0:T(8,128)} custom-call(f32[8,520,128]{2,1,0:T(8,128)} %copy-done, f32[4096,128]{1,0:T(8,128)} %get-tuple-element.71.items.block), custom_call_target="tpu_custom_call" | custom-call | tf_op jit(solution)/shard_map/share_0/pallas_call | solution.py:185
  178.7 3.0 %copy.20 = f32[4096,128]{1,0:T(8,128)} copy(f32[4096,128]{1,0:T(8,128)} %share_0.1) | data formatting | bytes 4194304
Async XLA Ops:
  2.0 1.6 copy-start.1
  3.6 0.7 copy-start.2
  4.3 0.7 copy-start.4
  22.6 70.1 %copy-start.3 = (s32[2,256]{1,0:T(2,128)S(1)}, s32[2,256]{1,0:T(2,128)}, u32[]{:S(2)}) copy-start(s32[2,256]{1,0:T(2,128)} %ut.3) | copy-start | bytes 6148
  22.6 70.1 %copy-start.5 = (s32[2,256]{1,0:T(2,128)S(1)}, s32[2,256]{1,0:T(2,128)}, u32[]{:S(2)}) copy-start(s32[2,256]{1,0:T(2,128)} %it.3) | copy-start | bytes 6148
  104.6 1.3 copy-start

commit v2 on v1

v2 whole, which is shorter than its diff:
```python
import functools

import jax
import jax.numpy as jnp
from jax import lax
from jax.experimental import pallas as pl
from jax.experimental.pallas import tpu as pltpu
from jax.sharding import PartitionSpec as P

LR = 0.05
KEEP = 1.0 - 0.05*0.05
NT = (((1,), (1,)), ((), ()))
NN = (((1,), (0,)), ((), ()))
f32, bf16 = jnp.float32, jnp.bfloat16

def tile_kernel(epoch, slots, shards, chunks, group,
                ut, it, live_ref, users, items, ratings,
                users_out, grads_out, counts_out,
                rat, uf, vf, ub, utb, vb, du, dv, cv_, su, si, rsem, msem):
    tiles = ub.shape[0]
    T = ub.shape[1]
    width = slots // chunks
    loads = [pltpu.make_async_copy(ratings.at[epoch, pl.ds(c*width, width)], rat.at[pl.ds(c*width, width)], rsem.at[c]) for c in range(chunks)]
    cu = pltpu.make_async_copy(users, uf, msem.at[0])
    cv = pltpu.make_async_copy(items, vf, msem.at[1])
    cu.start(); cv.start()
    for l in loads: l.start()

    @pl.loop(0, tiles)
    def _(b):
        su[b] = 0
        si[b] = 0
        du[b] = jnp.zeros((T, T), f32)
        dv[b] = jnp.zeros((T, T), f32)
    eye = (lax.broadcasted_iota(jnp.int32, (T, T), 0) == lax.broadcasted_iota(jnp.int32, (T, T), 1)).astype(bf16)
    cu.wait()
    @pl.loop(0, tiles, step=4)
    def _(b0):
        for k in range(4):
            b = b0 + k
            x = uf[pl.ds(b*T, T), :].astype(bf16)
            ub[b] = x
            utb[b] = lax.dot_general(eye, x, NT, preferred_element_type=f32).astype(bf16)
    cv.wait()
    @pl.loop(0, tiles, step=4)
    def _(b0):
        for k in range(4):
            b = b0 + k
            vb[b] = vf[pl.ds(b*T, T), :].astype(bf16)
    live = live_ref[epoch, 0]

    for c in range(chunks):
        loads[c].wait()
        base = c*width
        count = jnp.clip(live - base, 0, width)
        @pl.loop(0, pl.cdiv(count, group))
        def _(j):
            t0 = base + j*group
            aa, bb, rr = [], [], []
            for k in range(group):
                t = t0 + k
                a = ut[epoch, t]; b = it[epoch, t]
                aa.append(a); bb.append(b)
            for k in range(group):
                t = t0 + k
                p = lax.dot_general(ub[aa[k]], vb[bb[k]], NT, preferred_element_type=f32)
                r = rat[t].astype(f32) - p
                if k:
                    r = jnp.where(t < live, r, 0.0)
                rr.append(r.astype(bf16))
            gu = [lax.dot_general(rr[k], vb[bb[k]], NN, preferred_element_type=f32) for k in range(group)]
            gv = [lax.dot_general(utb[aa[k]], rr[k], NN, preferred_element_type=f32) for k in range(group)]
            for k in range(group):
                one = (t0 + k < live).astype(jnp.int32)
                du[aa[k]] += gu[k]
                dv[bb[k]] += gv[k]
                su[aa[k]] = su[aa[k]] + one
                si[bb[k]] = si[bb[k]] + one
    row = lax.broadcasted_iota(jnp.int32, (8, T), 0)
    for r in range(shards):
        x, hy = r // 2, r % 2
        lo, hi = x % 2, x // 2
        z = jnp.zeros((8, T), f32)
        for d in range(2):
            for c in range(2):
                b = (d*2+c)*8 + (hi if d else lo ^ hi)*4 + hy*2 + lo
                z = jnp.where(row == d*2+c, si[b].astype(f32), z)
        cv_[r] = z
    oc = pltpu.make_async_copy(cv_, counts_out, msem.at[4])
    oc.start()
    og = pltpu.make_async_copy(dv, grads_out, msem.at[2])
    og.start()
    @pl.loop(0, tiles, step=2)
    def _(b0):
        for k in range(2):
            b = b0 + k
            cnt = jnp.full((1, T), jnp.maximum(su[b], 1), jnp.int32).astype(f32)
            sl = pl.ds(pl.multiple_of(b*T, T), T)
            uf[sl, :] = uf[sl, :]*KEEP + du[b]*(LR/cnt)
    ou = pltpu.make_async_copy(uf, users_out, msem.at[3])
    ou.start()
    og.wait(); ou.wait(); oc.wait()

def tiles_step(epoch, ut, it, live, users, items, ratings, shards=8, chunks=8, group=16):
    slots, T = ratings.shape[1], ratings.shape[2]
    tiles = users.shape[0]//T
    smem = pl.BlockSpec(memory_space=pltpu.SMEM)
    anyb = pl.BlockSpec(memory_space=pl.ANY)
    return pl.pallas_call(
        functools.partial(tile_kernel, epoch, slots, shards, chunks, group),
        out_shape=(jax.ShapeDtypeStruct(users.shape, f32), jax.ShapeDtypeStruct((tiles, T, T), f32), jax.ShapeDtypeStruct((shards, 8, T), f32)),
        in_specs=[smem]*3+[anyb]*3, out_specs=(anyb,)*3,
        scratch_shapes=[pltpu.VMEM((slots,T,T),bf16), pltpu.VMEM(users.shape,f32), pltpu.VMEM(items.shape,f32),
            pltpu.VMEM((tiles,T,T),bf16),pltpu.VMEM((tiles,T,T),bf16),pltpu.VMEM((tiles,T,T),bf16),
            pltpu.VMEM((tiles,T,T),f32), pltpu.VMEM((tiles,T,T),f32), pltpu.VMEM((shards,8,T),f32),
            pltpu.SMEM((tiles,),jnp.int32),pltpu.SMEM((tiles,),jnp.int32),
            pltpu.SemaphoreType.DMA((chunks,)), pltpu.SemaphoreType.DMA((5,))],
        compiler_params=pltpu.CompilerParams(vmem_limit_bytes=48<<20),
        name="tile_step",
    )(ut, it, live, users, items, ratings)


MESH = pl.DeviceIdType.MESH


def share_kernel(mask, grads, counts, block, out, acc, old, new, rx1, ry, rx2, cin, cmine,
                 s1, r1, sy, ry_s, s2, r2, sc, rc, se, re, t2, q2, ty, qy, t1, q1, lsem):
    T = block.shape[1]
    n = counts.shape[0]
    s = lax.axis_index("stratum")
    r = lax.axis_index("replica")
    x, hy = lax.div(r, 2), lax.rem(r, 2)
    lo, hi = lax.rem(x, 2), lax.div(x, 2)
    xa = x + 1 - 2 * lo
    xb = 3 - x
    at = lambda x_, y_: (s, x_ * 2 + y_)
    first = (at(xa, hy), at(xb, hy))
    second = (at(xb, hy), at(xa, hy))
    over = at(x, 1 - hy)
    h1 = (lo + hi - 2 * lo * hi, hi)
    h2 = (lo, lo)

    def tile(d, c, a, b, e):
        return (d * 2 + c) * 8 + a * 4 + b * 2 + e

    def put(src, dst, ss, rs, dev):
        cp = pltpu.make_async_remote_copy(src_ref=src, dst_ref=dst, send_sem=ss, recv_sem=rs, device_id=dev, device_id_type=MESH)
        cp.start()
        return cp

    def rows(b):
        return pl.ds(pl.multiple_of(b * T, T), T)

    bar = pltpu.get_barrier_semaphore()
    for k in range(1, n):
        pl.semaphore_signal(bar, inc=1, device_id=(s, lax.rem(r + k, n)), device_id_type=MESH)
    across = s
    if mask:
        for bit in range(4):
            if mask >> bit & 1:
                across = across + (1 << bit) - (2 << bit) * lax.rem(lax.div(s, 1 << bit), 2)
        pl.semaphore_signal(bar, inc=1, device_id=(across, r), device_id_type=MESH)
    local = [pltpu.make_async_copy(grads, acc, lsem.at[0]), pltpu.make_async_copy(counts.at[r], cmine, lsem.at[1])]
    mine = {}
    for d in range(2):
        for c in range(2):
            b = tile(d, c, h1[d], hy, h2[d])
            mine[d, c] = b
            local.append(pltpu.make_async_copy(block.at[rows(b)], old.at[d, c], lsem.at[2 + d * 2 + c]))
    for cp in local:
        cp.start()
    pl.semaphore_wait(bar, n - 1 + (1 if mask else 0))

    pend = []
    got1, goty, got2, gote = {}, {}, {}, {}
    for half in range(2):
        for c in range(2):
            for e in range(2):
                for d in range(2):
                    i = half * 2 + e
                    yb = hy if half else 1 - hy
                    eb = 1 - h2[d] if e else h2[d]
                    got1[d, c, i] = put(grads.at[tile(d, c, 1 - h1[d], yb, eb)], rx1.at[d, c, i], s1.at[d, c, i], r1.at[d, c, i], first[d])
        if not half:
            gotc = [put(counts.at[lax.rem(r + k, n)], cin.at[k - 1], sc.at[k - 1], rc.at[k - 1], (s, lax.rem(r + k, n))) for k in range(1, n)]
    for cp in local:
        cp.wait()

    def add(d, c, a, b, e, part):
        acc[tile(d, c, a, b, e)] += part[...]

    def take1(c, i):
        for d in range(2):
            e = h2[d] if i % 2 else 1 - h2[d]
            b = hy if i >= 2 else 1 - hy
            got1[d, c, i].wait_recv()
            add(d, c, h1[d], b, e, rx1.at[d, c, i])
            if i < 2:
                goty[d, c, i] = put(acc.at[tile(d, c, h1[d], b, e)], ry.at[d, c, i], sy.at[d, c, i], ry_s.at[d, c, i], over)

    def takey(c, j):
        for d in range(2):
            e = h2[d] if j else 1 - h2[d]
            goty[d, c, j].wait_recv()
            add(d, c, h1[d], hy, e, ry.at[d, c, j])
            if j == 0:
                got2[d, c] = put(acc.at[tile(d, c, h1[d], hy, e)], rx2.at[d, c], s2.at[d, c], r2.at[d, c], second[d])

    own = {}
    def finish(c):
        for d in range(2):
            b = mine[d, c]
            got2[d, c].wait_recv()
            total = acc[b] + rx2[d, c]
            cnt = jnp.maximum(cmine[pl.ds(d * 2 + c, 1), :], 1.0)
            fresh = old[d, c] * KEEP + total.T * (LR / cnt)
            if mask:
                new[d, c] = fresh
                gote[d, c] = put(new.at[d, c], out.at[rows(b)], se.at[d, c], re.at[d, c], (across, r))
            else:
                out[rows(b), :] = fresh

    ag2, agy, ag1 = {}, {}, {}

    def send2(d, c, b):
        ag2[d, c] = put(out.at[rows(b)], out.at[rows(b)], t2.at[d, c], q2.at[d, c], second[d])

    def sendy(d, c, j, b):
        agy[d, c, j] = put(out.at[rows(b)], out.at[rows(b)], ty.at[d, c, j], qy.at[d, c, j], over)

    def send1(d, c, i, b):
        ag1[d, c, i] = put(out.at[rows(b)], out.at[rows(b)], t1.at[d, c, i], q1.at[d, c, i], first[d])

    def spread(c):
        for d in range(2):
            b = mine[d, c]
            if mask:
                gote[d, c].wait_recv()
            send2(d, c, b)
            sendy(d, c, 0, b)
            send1(d, c, 0, b)

    def pass2(c):
        for d in range(2):
            ag2[d, c].wait_recv()
            b = tile(d, c, h1[d], hy, 1 - h2[d])
            sendy(d, c, 1, b)
            send1(d, c, 1, b)

    def passy(c, j):
        for d in range(2):
            agy[d, c, j].wait_recv()
            b = tile(d, c, h1[d], 1 - hy, 1 - h2[d] if j else h2[d])
            send1(d, c, 2 + j, b)

    for c in range(2):
        take1(c, 0)
        take1(c, 1)
    for g in gotc:
        g.wait_recv()
    cmine[...] += functools.reduce(lambda p, q: p + q, [cin[k] for k in range(n - 1)])
    take1(0, 2)
    take1(0, 3)
    takey(0, 0)
    takey(0, 1)
    take1(1, 2)
    finish(0)
    take1(1, 3)
    takey(1, 0)
    spread(0)
    takey(1, 1)
    finish(1)
    pass2(0)
    passy(0, 0)
    spread(1)
    passy(0, 1)
    pass2(1)
    passy(1, 0)
    passy(1, 1)
    for table in (got1, goty, got2, gote):
        for cp in table.values():
            cp.wait_send()
    for g in gotc:
        g.wait_send()
    for table in (ag2, agy):
        for cp in table.values():
            cp.wait_send()
    for cp in ag1.values():
        cp.wait()


def share(grads, counts, block, mask, cid):
    tiles, T = grads.shape[0], grads.shape[1]
    n = counts.shape[0]
    anyb = pl.BlockSpec(memory_space=pl.ANY)
    dma = lambda *k: pltpu.SemaphoreType.DMA(k)
    both = lambda *k: [dma(*k), dma(*k)]
    return pl.pallas_call(
        functools.partial(share_kernel, mask),
        out_shape=pltpu.VMEM(block.shape, f32),
        in_specs=[anyb] * 3,
        out_specs=pl.BlockSpec(memory_space=pltpu.VMEM),
        scratch_shapes=[
            pltpu.VMEM((tiles, T, T), f32),
            pltpu.VMEM((2, 2, T, T), f32),
            pltpu.VMEM((2, 2, T, T), f32),
            pltpu.VMEM((2, 2, 4, T, T), f32),
            pltpu.VMEM((2, 2, 2, T, T), f32),
            pltpu.VMEM((2, 2, T, T), f32),
            pltpu.VMEM((n - 1, 8, T), f32),
            pltpu.VMEM((8, T), f32),
            *both(2, 2, 4), *both(2, 2, 2), *both(2, 2), *both(n - 1), *both(2, 2),
            *both(2, 2), *both(2, 2, 2), *both(2, 2, 4), dma(6),
        ],
        compiler_params=pltpu.CompilerParams(collective_id=cid, has_side_effects=True, vmem_limit_bytes=24 << 20),
        name=f"share_{mask}",
    )(grads, counts, block)


def local(user_factors, item_factors, ratings, user_tile, item_tile, live_count, partner):
    n = lax.axis_size("replica")
    half = lax.axis_size("stratum") // 2
    users, grads, counts = tiles_step(0, user_tile, item_tile, live_count, user_factors, item_factors, ratings, n)
    branches = [functools.partial(share, mask=half + k, cid=1 + k) for k in range(half)]
    block = lax.switch(partner[0] - half, branches, grads, counts, item_factors)
    users, grads, counts = tiles_step(1, user_tile, item_tile, live_count, users, block, ratings, n)
    return users, share(grads, counts, block, 0, 0)


def solution(mesh):
    return jax.shard_map(
        local,
        mesh=mesh,
        in_specs=(
            P(("stratum", "replica"), None),
            P("stratum", None),
            P(None, ("stratum", "replica"), None, None),
            P(None, ("stratum", "replica")),
            P(None, ("stratum", "replica")),
            P(None, ("stratum", "replica")),
            P(),
        ),
        out_specs=(P(("stratum", "replica"), None), P("stratum", None)),
        check_vma=False,
    )
```

time: 182 us -> 134 us (0.74)
  the two profiles are of different devices: /device:TPU:60 before, /device:TPU:0 now
where the time goes in v2:
time: 134 us; the launch traced here: 133 us
  Pallas kernels  124 us (93%)
  local copies, waits for them, and re-layouts  7.93 us (6%)
  between operations  1.35 us (1%)
    pallas_call x2, Pallas kernels, share(): pl.pallas_call(functools.partial(share_kernel, mask), out_shape=pltpu.VME...  96.3 us
    pallas_call x2, Pallas kernels, tiles_step(): pl.pallas_call(functools.partial(tile_kernel, epoch, slots, shards, chunk...  27.6 us
    unnamed x18, local copies, waits for them, and re-layouts  7.93 us

profile of v2, /device:TPU:0, one launch (start us, length us, event | category | flops | bytes accessed | tf_op | source)
XLA Modules:
  0.0 133.4 jit_solution(14177208236093674384)
XLA Ops:
  1.3 0.7 copy.10.live_ref
  2.0 0.0 copy-start
  2.0 1.6 %copy-done = f32[4096,128]{1,0:T(8,128)S(1)} copy-done((f32[4096,128]{1,0:T(8,128)S(1)}, f32[4096,128]{1,0:T(8,128)}, u32[]{:S(2)}) %copy-start) | copy-done | bytes 2097176
  3.6 0.0 copy-start.3
  3.6 0.7 copy-done.3
  4.3 0.0 copy-start.5
  4.3 0.7 copy-done.5
  5.0 0.0 copy-start.7
  5.0 15.3 %tile_step.2 = (f32[4096,128]{1,0:T(8,128)S(1)}, f32[32,128,128]{2,1,0:T(8,128)S(1)}, f32[8,8,128]{2,1,0:T(8,128)S(1)}) custom-call(s32[2,256]{1,0:T(2,128)S(1)} %copy-done.3, s32[2,256]{1,0:T(2,128)S(1)} %copy-done.5, s32[2,1]{1,0:T(2,128)S(1)} %copy.10.live_ref, f32[4096,128]{1,0:T(8,128)S(1)} %copy-done, f32[4096,128]{1,0:T(8,128)} %items.1, ...), custom_call_target="tpu_custom_call" | custom-call | tf_op jit(solution)/shard_map/tile_step/pallas_call | solution.py:109
  20.3 0.0 copy-start.1
  20.3 1.3 copy-done.1
  21.6 0.0 copy-done.7
  21.6 0.0 copy-start.4
  21.6 0.0 copy-start.6
  21.6 50.6 %conditional.1 = (f32[4096,128]{1,0:T(8,128)S(1)}) conditional(s32[]{:T(128)} %bitcast, (f32[32,128,128]{2,1,0:T(8,128)S(1)}, f32[8,8,128]{2,1,0:T(8,128)S(1)}, f32[4096,128]{1,0:T(8,128)S(1)}) %tuple.44, (f32[32,128,128]{2,1,0:T(8,128)S(1)}, f32[8,8,128]{2,1,0:T(8,128)S(1)}, f32[4096,128]{1,0:T(8,128)S(1)}) %tuple.45, ...), branch_computations={%region_0.0_spmd, %region_1.0_spmd, %region_2.0_spmd, %region_3.0_... | conditional | bytes 8 | solution.py:325
  21.6 50.4 %share_11.1 = f32[4096,128]{1,0:T(8,128)S(1)} custom-call(f32[32,128,128]{2,1,0:T(8,128)S(1)} %get-tuple-element.66.grads, f32[8,8,128]{2,1,0:T(8,128)S(1)} %get-tuple-element.67.counts, f32[4096,128]{1,0:T(8,128)S(1)} %get-tuple-element.68.block), custom_call_target="tpu_custom_call" | custom-call | tf_op jit(solution)/shard_map/cond/branch_3_fun/share_11/pallas_call | solution.py:298
  72.3 0.0 copy-done.4
  72.3 0.0 copy-done.6
  72.3 0.0 copy-start.2
  72.3 1.6 %copy-done.2 = f32[4096,128]{1,0:T(8,128)S(1)} copy-done((f32[4096,128]{1,0:T(8,128)S(1)}, f32[4096,128]{1,0:T(8,128)}, u32[]{:S(2)}) %copy-start.2) | copy-done | bytes 2097176
  73.9 12.3 %tile_step.3 = (f32[4096,128]{1,0:T(8,128)}, f32[32,128,128]{2,1,0:T(8,128)S(1)}, f32[8,8,128]{2,1,0:T(8,128)S(1)}) custom-call(s32[2,256]{1,0:T(2,128)S(1)} %copy-done.4, s32[2,256]{1,0:T(2,128)S(1)} %copy-done.6, s32[2,1]{1,0:T(2,128)S(1)} %copy.10.live_ref, f32[4096,128]{1,0:T(8,128)S(1)} %copy-done.2, f32[4096,128]{1,0:T(8,128)S(1)} %get-tuple-element.99.items.block, ...), custom_call_target="tpu_custom_call" | custom-call | tf_op jit(solution)/shard_map/tile_step/pallas_call | solution.py:109
  86.2 45.9 %share_0.1 = f32[4096,128]{1,0:T(8,128)S(1)} custom-call(f32[32,128,128]{2,1,0:T(8,128)S(1)} %get-tuple-element.93.grads, f32[8,8,128]{2,1,0:T(8,128)S(1)} %get-tuple-element.94.counts, f32[4096,128]{1,0:T(8,128)S(1)} %get-tuple-element.99.items.block), custom_call_target="tpu_custom_call" | custom-call | tf_op jit(solution)/shard_map/share_0/pallas_call | solution.py:298
  132.1 1.3 copy.20
Async XLA Ops:
  2.0 1.6 %copy-start = (f32[4096,128]{1,0:T(8,128)S(1)}, f32[4096,128]{1,0:T(8,128)}, u32[]{:S(2)}) copy-start(f32[4096,128]{1,0:T(8,128)} %users.1) | copy-start | bytes 6291460
  3.6 0.7 copy-start.3
  4.3 0.7 copy-start.5
  5.0 16.6 %copy-start.7 = (f32[4096,128]{1,0:T(8,128)S(1)}, f32[4096,128]{1,0:T(8,128)}, u32[]{:S(2)}) copy-start(f32[4096,128]{1,0:T(8,128)} %items.1) | copy-start | bytes 6291460
  20.3 1.3 copy-start.1
  21.6 50.7 %copy-start.4 = (s32[2,256]{1,0:T(2,128)S(1)}, s32[2,256]{1,0:T(2,128)}, u32[]{:S(2)}) copy-start(s32[2,256]{1,0:T(2,128)} %ut.3) | copy-start | bytes 6148
  21.6 50.7 %copy-start.6 = (s32[2,256]{1,0:T(2,128)S(1)}, s32[2,256]{1,0:T(2,128)}, u32[]{:S(2)}) copy-start(s32[2,256]{1,0:T(2,128)} %it.3) | copy-start | bytes 6148
  72.3 1.6 %copy-start.2 = (f32[4096,128]{1,0:T(8,128)S(1)}, f32[4096,128]{1,0:T(8,128)}, u32[]{:S(2)}) copy-start(f32[4096,128]{1,0:T(8,128)} %copy-done.1) | copy-start | bytes 6291460

commit v3 on v2

v3 whole, which is shorter than its diff:
```python
import functools

import jax
import jax.numpy as jnp
from jax import lax
from jax.experimental import pallas as pl
from jax.experimental.pallas import tpu as pltpu
from jax.sharding import PartitionSpec as P

LR = 0.05
KEEP = 1.0 - 0.05 * 0.05
NT = (((1,), (1,)), ((), ()))
NN = (((1,), (0,)), ((), ()))
f32, bf16, i32 = jnp.float32, jnp.bfloat16, jnp.int32
GROUP = 16


def pin(x, space=pltpu.HBM):
    return pltpu.with_memory_space_constraint(x, space)


def tile_kernel(epoch, shards, chunks, ut_in, it_in, live_in, users, items, ratings,
                users_out, dv, counts_out,
                ut, it, live_ref, rat, uf, vf, ub, utb, vb, du,
                rbuf, pa, p1, p2, nb, pend, su, si, rsem, msem, osem):
    tiles, T = ub.shape[0], ub.shape[1]
    slots = rat.shape[0]
    width = slots // chunks
    first = epoch == 0
    per = slots // tiles

    def load(c):
        o = pl.ds(c * width, width)
        return pltpu.make_async_copy(ratings.at[epoch, o], rat.at[o], rsem.at[c])

    def rows(b):
        return pl.ds(pl.multiple_of(b * T, T), T)

    small = [pltpu.make_async_copy(ut_in, ut, msem.at[0]), pltpu.make_async_copy(it_in, it, msem.at[1]),
             pltpu.make_async_copy(live_in, live_ref, msem.at[2])]
    big = [pltpu.make_async_copy(users, uf, msem.at[3]), pltpu.make_async_copy(items, vf, msem.at[4])]
    for cp in small + big:
        cp.start()
    for c in range(chunks):
        load(c).start()

    @pl.loop(0, tiles)
    def _(b):
        su[b] = 0
        si[b] = 0
        pend[b] = -1
        du[b] = jnp.zeros((T, T), f32)
        dv[b] = jnp.zeros((T, T), f32)

    for cp in small + big:
        cp.wait()
    live = live_ref[epoch, 0]
    eye = (lax.broadcasted_iota(i32, (T, T), 0) == lax.broadcasted_iota(i32, (T, T), 1)).astype(bf16)

    @functools.partial(lax.fori_loop, 0, tiles // 2, init_val=jnp.int32(GROUP))
    def pairs(i, np):
        for k in range(2):
            b = i * 2 + k
            x = uf[rows(b), :].astype(bf16)
            ub[b] = x
            utb[b] = lax.dot_general(eye, x, NT, preferred_element_type=f32).astype(bf16)
            vb[b] = vf[rows(b), :].astype(bf16)
        for k in range(2 * per):
            t = i * (2 * per) + k
            a, b = ut[epoch, t], it[epoch, t]
            valid = t < live
            q = pend[a]
            has = jnp.logical_and(valid, q >= 0)
            pa[np] = a
            p1[np] = q
            p2[np] = t
            np = np + has.astype(i32)
            pend[a] = jnp.where(valid, jnp.where(has, -1, t), q)
            one = valid.astype(i32)
            su[a] = su[a] + one
            si[b] = si[b] + one
        nb[i] = np
        return np

    @functools.partial(lax.fori_loop, 0, tiles, init_val=pairs)
    def total(a, np):
        q = pend[a]
        pa[np] = a
        p1[np] = q
        p2[np] = -1
        return np + (q >= 0).astype(i32)

    for k in range(GROUP):
        for o in (0, total):
            pa[o + k] = 0
            p1[o + k] = -1
            p2[o + k] = -1

    rbuf[...] = jnp.zeros(rbuf.shape, bf16)

    def names(g):
        out = []
        for k in range(GROUP):
            p = g * GROUP + k
            x, y = p1[p], p2[p]
            tx, ty = jnp.maximum(x, 0), jnp.maximum(y, 0)
            out.append((pa[p], x, y, tx, ty, it[epoch, tx], it[epoch, ty]))
        return out

    def flush(g):
        todo = names(g)
        gu, gv = [], []
        for k, (a, x, y, tx, ty, bx, by) in enumerate(todo):
            r = rbuf[k]
            v = jnp.concatenate([vb[bx], vb[by]], axis=0)
            gu.append(lax.dot_general(r, v, NN, preferred_element_type=f32))
            gv.append(lax.dot_general(utb[a], r, NN, preferred_element_type=f32))
        return todo, gu, gv

    def fill(g):
        res = []
        for k, (a, x, y, tx, ty, bx, by) in enumerate(names(g)):
            v = jnp.concatenate([vb[bx], vb[by]], axis=0)
            p = lax.dot_general(ub[a], v, NT, preferred_element_type=f32)
            r1 = (rat[tx].astype(f32) - p[:, :T]).astype(bf16)
            r2 = (rat[ty].astype(f32) - p[:, T:]).astype(bf16)
            zero = jnp.zeros((T, T), bf16)
            res.append(jnp.concatenate([jnp.where(x >= 0, r1, zero), jnp.where(y >= 0, r2, zero)], axis=1))
        return res

    def settle(todo, gu, gv):
        for k, (a, x, y, tx, ty, bx, by) in enumerate(todo):
            du[a] += gu[k]
            dv[bx] += gv[k][:, :T]
            dv[by] += gv[k][:, T:]

    def work(g, carry):
        todo, gu, gv = flush(g)
        res = fill(g + 1)
        for k in range(GROUP):
            rbuf[k] = res[k]
        settle(todo, gu, gv)
        return carry

    def chunk(c, done):
        load(c).wait()
        upto = nb[(c + 1) * (tiles // 2 // chunks) - 1] // GROUP - 1
        upto = jnp.where(c == chunks - 1, pl.cdiv(total, GROUP) - 1, upto)
        lax.fori_loop(done, upto, work, 0)
        return jnp.maximum(done, upto)

    ended = lax.fori_loop(0, chunks, chunk, jnp.int32(0))
    settle(*flush(ended))

    row = lax.broadcasted_iota(i32, (8, T), 0)
    for r in range(shards):
        x, hy = r // 2, r % 2
        lo, hi = x % 2, x // 2
        z = jnp.zeros((8, T), f32)
        for d in range(2):
            for c in range(2):
                b = (d * 2 + c) * 8 + (hi if d else lo ^ hi) * 4 + hy * 2 + lo
                z = jnp.where(row == d * 2 + c, si[b].astype(f32), z)
        counts_out[r] = z


    def update(i, carry):
        for k in range(2):
            b = i * 2 + k
            cnt = jnp.full((1, T), jnp.maximum(su[b], 1), i32).astype(f32)
            uf[rows(b), :] = uf[rows(b), :] * KEEP + du[b] * (LR / cnt)
        return carry

    quarter = tiles // 4
    sent = []
    for part in range(4):
        lax.fori_loop(part * quarter // 2, (part + 1) * quarter // 2, update, 0)
        o = pl.ds(part * quarter * T, quarter * T)
        sent.append(pltpu.make_async_copy(uf.at[o], users_out.at[o], osem.at[part]))
        sent[-1].start()
    for cp in sent:
        cp.wait()


def tiles_step(epoch, ut, it, live, users, items, ratings, shards=8, chunks=8):
    slots, T = ratings.shape[1], ratings.shape[2]
    tiles = users.shape[0] // T
    first = epoch == 0
    hbm = pl.BlockSpec(memory_space=pltpu.HBM)
    vmem = pl.BlockSpec(memory_space=pltpu.VMEM)
    smem = lambda *k: pltpu.SMEM(k, i32)
    length = slots // 2 + tiles + 2 * GROUP
    return pl.pallas_call(
        functools.partial(tile_kernel, epoch, shards, chunks),
        out_shape=(pltpu.HBM(users.shape, f32), pltpu.VMEM((tiles, T, T), f32), pltpu.VMEM((shards, 8, T), f32)),
        in_specs=[hbm] * 4 + [hbm if first else pl.BlockSpec(memory_space=pl.ANY)] + [hbm],
        out_specs=(hbm, vmem, vmem),
        scratch_shapes=[
            smem(*ut.shape), smem(*it.shape), smem(*live.shape),
            pltpu.VMEM((slots, T, T), bf16),
            pltpu.VMEM(users.shape, f32),
            pltpu.VMEM(items.shape, f32),
            pltpu.VMEM((tiles, T, T), bf16), pltpu.VMEM((tiles, T, T), bf16), pltpu.VMEM((tiles, T, T), bf16),
            pltpu.VMEM((tiles, T, T), f32),
            pltpu.VMEM((GROUP, T, 2 * T), bf16),
            smem(length), smem(length), smem(length), smem(tiles // 2), smem(tiles), smem(tiles), smem(tiles),
            pltpu.SemaphoreType.DMA((chunks,)), pltpu.SemaphoreType.DMA((5,)), pltpu.SemaphoreType.DMA((4,)),
        ],
        compiler_params=pltpu.CompilerParams(vmem_limit_bytes=32 << 20),
        name=f"tile_step_{epoch}",
    )(pin(ut), pin(it), pin(live), pin(users), pin(items) if first else items, pin(ratings))


MESH = pl.DeviceIdType.MESH


def share_kernel(mask, grads, counts, block, dest, hold, acc, old, new, rx1, ry, rx2, cin, cmine,
                 s1, r1, sy, ry_s, s2, r2, sc, rc, se, re, t2, q2, ty, qy, t1, q1, lsem, wsem):
    T = block.shape[1]
    n = counts.shape[0]
    s = lax.axis_index("stratum")
    r = lax.axis_index("replica")
    x, hy = lax.div(r, 2), lax.rem(r, 2)
    lo, hi = lax.rem(x, 2), lax.div(x, 2)
    xa = x + 1 - 2 * lo
    xb = 3 - x
    at = lambda x_, y_: (s, x_ * 2 + y_)
    first = (at(xa, hy), at(xb, hy))
    second = (at(xb, hy), at(xa, hy))
    over = at(x, 1 - hy)
    h1 = (lo + hi - 2 * lo * hi, hi)
    h2 = (lo, lo)

    def tile(d, c, a, b, e):
        return (d * 2 + c) * 8 + a * 4 + b * 2 + e

    def put(src, dst, ss, rs, dev):
        cp = pltpu.make_async_remote_copy(src_ref=src, dst_ref=dst, send_sem=ss, recv_sem=rs, device_id=dev, device_id_type=MESH)
        cp.start()
        return cp

    def rows(b):
        return pl.ds(pl.multiple_of(b * T, T), T)

    out = hold if mask else dest
    saved = []

    def save(b):
        if mask:
            saved.append(pltpu.make_async_copy(out.at[rows(b)], dest.at[rows(b)], wsem.at[len(saved)]))
            saved[-1].start()

    bar = pltpu.get_barrier_semaphore()
    for k in range(1, n):
        pl.semaphore_signal(bar, inc=1, device_id=(s, lax.rem(r + k, n)), device_id_type=MESH)
    across = s
    if mask:
        for bit in range(4):
            if mask >> bit & 1:
                across = across + (1 << bit) - (2 << bit) * lax.rem(lax.div(s, 1 << bit), 2)
        pl.semaphore_signal(bar, inc=1, device_id=(across, r), device_id_type=MESH)
    local = [pltpu.make_async_copy(counts.at[r], cmine, lsem.at[1])]
    mine = {}
    for d in range(2):
        for c in range(2):
            b = tile(d, c, h1[d], hy, h2[d])
            mine[d, c] = b
            local.append(pltpu.make_async_copy(block.at[rows(b)], old.at[d, c], lsem.at[2 + d * 2 + c]))
    for cp in local:
        cp.start()
    pl.semaphore_wait(bar, n - 1 + (1 if mask else 0))

    pend = []
    got1, goty, got2, gote = {}, {}, {}, {}
    for half in range(2):
        for c in range(2):
            for e in range(2):
                for d in range(2):
                    i = half * 2 + e
                    yb = hy if half else 1 - hy
                    eb = 1 - h2[d] if e else h2[d]
                    got1[d, c, i] = put(grads.at[tile(d, c, 1 - h1[d], yb, eb)], rx1.at[d, c, i], s1.at[d, c, i], r1.at[d, c, i], first[d])
        if not half:
            gotc = [put(counts.at[lax.rem(r + k, n)], cin.at[k - 1], sc.at[k - 1], rc.at[k - 1], (s, lax.rem(r + k, n))) for k in range(1, n)]
    for cp in local:
        cp.wait()

    def add(d, c, a, b, e, part):
        t = tile(d, c, a, b, e)
        acc[t] = acc[t] + part[...]

    def take1(c, i):
        for d in range(2):
            e = h2[d] if i % 2 else 1 - h2[d]
            b = hy if i >= 2 else 1 - hy
            got1[d, c, i].wait_recv()
            t = tile(d, c, h1[d], b, e)
            acc[t] = grads[t] + rx1[d, c, i]
            if i < 2:
                goty[d, c, i] = put(acc.at[tile(d, c, h1[d], b, e)], ry.at[d, c, i], sy.at[d, c, i], ry_s.at[d, c, i], over)

    def takey(c, j):
        for d in range(2):
            e = h2[d] if j else 1 - h2[d]
            goty[d, c, j].wait_recv()
            add(d, c, h1[d], hy, e, ry.at[d, c, j])
            if j == 0:
                got2[d, c] = put(acc.at[tile(d, c, h1[d], hy, e)], rx2.at[d, c], s2.at[d, c], r2.at[d, c], second[d])

    own = {}
    def finish(c):
        for d in range(2):
            b = mine[d, c]
            got2[d, c].wait_recv()
            total = acc[b] + rx2[d, c]
            cnt = jnp.maximum(cmine[pl.ds(d * 2 + c, 1), :], 1.0)
            fresh = old[d, c] * KEEP + total.T * (LR / cnt)
            if mask:
                new[d, c] = fresh
                gote[d, c] = put(new.at[d, c], out.at[rows(b)], se.at[d, c], re.at[d, c], (across, r))
            else:
                out[rows(b), :] = fresh

    ag2, agy, ag1 = {}, {}, {}

    def send2(d, c, b):
        ag2[d, c] = put(out.at[rows(b)], out.at[rows(b)], t2.at[d, c], q2.at[d, c], second[d])

    def sendy(d, c, j, b):
        agy[d, c, j] = put(out.at[rows(b)], out.at[rows(b)], ty.at[d, c, j], qy.at[d, c, j], over)

    def send1(d, c, i, b):
        ag1[d, c, i] = put(out.at[rows(b)], out.at[rows(b)], t1.at[d, c, i], q1.at[d, c, i], first[d])

    def spread(c):
        for d in range(2):
            b = mine[d, c]
            if mask:
                gote[d, c].wait_recv()
            send2(d, c, b)
            sendy(d, c, 0, b)
            send1(d, c, 0, b)
            save(b)

    def pass2(c):
        for d in range(2):
            ag2[d, c].wait_recv()
            b = tile(d, c, h1[d], hy, 1 - h2[d])
            sendy(d, c, 1, b)
            send1(d, c, 1, b)
            save(b)

    def passy(c, j):
        for d in range(2):
            agy[d, c, j].wait_recv()
            b = tile(d, c, h1[d], 1 - hy, 1 - h2[d] if j else h2[d])
            send1(d, c, 2 + j, b)
            save(b)

    for c in range(2):
        take1(c, 0)
        take1(c, 1)
    for g in gotc:
        g.wait_recv()
    cmine[...] += functools.reduce(lambda p, q: p + q, [cin[k] for k in range(n - 1)])
    take1(0, 2)
    take1(0, 3)
    takey(0, 0)
    takey(0, 1)
    take1(1, 2)
    finish(0)
    take1(1, 3)
    takey(1, 0)
    spread(0)
    takey(1, 1)
    finish(1)
    pass2(0)
    passy(0, 0)
    spread(1)
    passy(0, 1)
    pass2(1)
    passy(1, 0)
    passy(1, 1)
    for c in range(2):
        for i in range(4):
            for d in range(2):
                ag1[d, c, i].wait_recv()
                save(tile(d, c, 1 - h1[d], 1 - hy if i >= 2 else hy, h2[d] if i % 2 else 1 - h2[d]))
    for table in (got1, goty, got2, gote, ag2, agy, ag1):
        for cp in table.values():
            cp.wait_send()
    for g in gotc:
        g.wait_send()
    for cp in saved:
        cp.wait()


def share(grads, counts, block, mask, cid):
    tiles, T = grads.shape[0], grads.shape[1]
    n = counts.shape[0]
    vmem = pl.BlockSpec(memory_space=pltpu.VMEM)
    hbm = pl.BlockSpec(memory_space=pltpu.HBM)
    dma = lambda *k: pltpu.SemaphoreType.DMA(k)
    both = lambda *k: [dma(*k), dma(*k)]
    return pl.pallas_call(
        functools.partial(share_kernel, mask),
        out_shape=(pltpu.HBM if mask else pltpu.VMEM)(block.shape, f32),
        in_specs=[vmem, vmem, hbm if mask else pl.BlockSpec(memory_space=pl.ANY)],
        out_specs=hbm if mask else vmem,
        scratch_shapes=[
            pltpu.VMEM(block.shape if mask else (8, T), f32),
            pltpu.VMEM((tiles, T, T), f32),
            pltpu.VMEM((2, 2, T, T), f32),
            pltpu.VMEM((2, 2, T, T), f32),
            pltpu.VMEM((2, 2, 4, T, T), f32),
            pltpu.VMEM((2, 2, 2, T, T), f32),
            pltpu.VMEM((2, 2, T, T), f32),
            pltpu.VMEM((n - 1, 8, T), f32),
            pltpu.VMEM((8, T), f32),
            *both(2, 2, 4), *both(2, 2, 2), *both(2, 2), *both(n - 1), *both(2, 2),
            *both(2, 2), *both(2, 2, 2), *both(2, 2, 4), dma(6), dma(tiles),
        ],
        compiler_params=pltpu.CompilerParams(collective_id=cid, has_side_effects=True, vmem_limit_bytes=24 << 20),
        name=f"share_{mask}",
    )(grads, counts, pin(block) if mask else block)


def local(user_factors, item_factors, ratings, user_tile, item_tile, live_count, partner):
    n = lax.axis_size("replica")
    half = lax.axis_size("stratum") // 2
    users, grads, counts = tiles_step(0, user_tile, item_tile, live_count, user_factors, item_factors, ratings, n)
    branches = [functools.partial(share, mask=half + k, cid=1 + k) for k in range(half)]
    block = lax.switch(partner[0] - half, branches, grads, counts, item_factors)
    users, grads, counts = tiles_step(1, user_tile, item_tile, live_count, users, block, ratings, n)
    return users, share(grads, counts, block, 0, 0)


def solution(mesh):
    return jax.shard_map(
        local,
        mesh=mesh,
        in_specs=(
            P(("stratum", "replica"), None),
            P("stratum", None),
            P(None, ("stratum", "replica"), None, None),
            P(None, ("stratum", "replica")),
            P(None, ("stratum", "replica")),
            P(None, ("stratum", "replica")),
            P(),
        ),
        out_specs=(P(("stratum", "replica"), None), P("stratum", None)),
        check_vma=False,
    )
```

time: 134 us -> 129 us (0.963)
  local copies, waits for them, and re-layouts: 7.93 us -> 2.62 us
    unnamed x18 -> x4, local copies, waits for them, and re-layouts: 7.93 us -> 2.62 us
where the time goes in v3:
time: 129 us; the launch traced here: 128 us
  Pallas kernels  123 us (95%)
  local copies, waits for them, and re-layouts  2.62 us (2%)
  between operations  1.33 us (1%)
    pallas_call x2, Pallas kernels, share(): pl.pallas_call(functools.partial(share_kernel, mask), out_shape=(pltpu.HB...  92.5 us
    pallas_call x2, Pallas kernels, tiles_step(): pl.pallas_call(functools.partial(tile_kernel, epoch, shards, chunks), out...  30.9 us
    unnamed x4, local copies, waits for them, and re-layouts  2.62 us

profile of v3, /device:TPU:0, one launch (start us, length us, event | category | flops | bytes accessed | tf_op | source)
XLA Modules:
  0.0 127.6 jit_solution(7489839167482711970)
XLA Ops:
  1.3 1.3 %copy.10.live_in = s32[2,1]{1,0:T(2,128)} copy(s32[2,1]{0,1:T(1,128)} %param.20) | data formatting | bytes 16 | tf_op args[5]
  2.6 15.9 %tile_step_0.1 = (f32[4096,128]{1,0:T(8,128)}, f32[32,128,128]{2,1,0:T(8,128)S(1)}, f32[8,8,128]{2,1,0:T(8,128)S(1)}) custom-call(s32[2,256]{1,0:T(2,128)} %ut_in.3, s32[2,256]{1,0:T(2,128)} %it_in.3, s32[2,1]{1,0:T(2,128)} %copy.10.live_in, f32[4096,128]{1,0:T(8,128)} %users.1, f32[4096,128]{1,0:T(8,128)} %items.1, bf16[2,256,128,128]{3,2,1,0:T(8,128)(2,1)} %ratings.3), custom_call_target="tpu_custom_call" | custom-call | tf_op jit(solution)/shard_map/tile_step_0/pallas_call | solution.py:193
  18.4 46.6 %conditional.1 = (f32[4096,128]{1,0:T(8,128)}) conditional(s32[]{:T(128)} %bitcast, (f32[32,128,128]{2,1,0:T(8,128)S(1)}, f32[8,8,128]{2,1,0:T(8,128)S(1)}, f32[4096,128]{1,0:T(8,128)}) %tuple.32, (f32[32,128,128]{2,1,0:T(8,128)S(1)}, f32[8,8,128]{2,1,0:T(8,128)S(1)}, f32[4096,128]{1,0:T(8,128)}) %tuple.32, ...), branch_computations={%region_0.0_spmd, %region_1.0_spmd, %region_2.0_spmd, %region_3.0_... | conditional | bytes 8 | solution.py:433
  18.5 46.3 %share_13.1 = f32[4096,128]{1,0:T(8,128)} custom-call(f32[32,128,128]{2,1,0:T(8,128)S(1)} %get-tuple-element.72.grads, f32[8,8,128]{2,1,0:T(8,128)S(1)} %get-tuple-element.73.counts, f32[4096,128]{1,0:T(8,128)} %get-tuple-element.74.block), custom_call_target="tpu_custom_call" | custom-call | tf_op jit(solution)/shard_map/cond/branch_5_fun/share_13/pallas_call | solution.py:405
  65.0 0.0 copy-start
  65.1 15.0 %tile_step_1.1 = (f32[4096,128]{1,0:T(8,128)}, f32[32,128,128]{2,1,0:T(8,128)S(1)}, f32[8,8,128]{2,1,0:T(8,128)S(1)}) custom-call(s32[2,256]{1,0:T(2,128)} %ut_in.3, s32[2,256]{1,0:T(2,128)} %it_in.3, s32[2,1]{1,0:T(2,128)} %copy.10.live_in, f32[4096,128]{1,0:T(8,128)} %get-tuple-element.89.users, f32[4096,128]{1,0:T(8,128)} %get-tuple-element.99.items.block, ...), custom_call_target="tpu_custom_call" | custom-call | tf_op jit(solution)/shard_map/tile_step_1/pallas_call | solution.py:193
  80.1 0.0 copy-done
  80.1 46.1 %share_0.1 = f32[4096,128]{1,0:T(8,128)S(1)} custom-call(f32[32,128,128]{2,1,0:T(8,128)S(1)} %get-tuple-element.93.grads, f32[8,8,128]{2,1,0:T(8,128)S(1)} %get-tuple-element.94.counts, f32[4096,128]{1,0:T(8,128)S(1)} %copy-done), custom_call_target="tpu_custom_call" | custom-call | tf_op jit(solution)/shard_map/share_0/pallas_call | solution.py:405
  126.2 1.3 %copy.20 = f32[4096,128]{1,0:T(8,128)} copy(f32[4096,128]{1,0:T(8,128)S(1)} %share_0.1) | data formatting | bytes 4194304
Async XLA Ops:
  65.0 15.0 %copy-start = (f32[4096,128]{1,0:T(8,128)S(1)}, f32[4096,128]{1,0:T(8,128)}, u32[]{:S(2)}) copy-start(f32[4096,128]{1,0:T(8,128)} %get-tuple-element.99.items.block) | copy-start | bytes 6291460

commit v4 on v3

--- a/solution.py
+++ b/solution.py
@@ -52,19 +52,12 @@
         du[b] = jnp.zeros((T, T), f32)
         dv[b] = jnp.zeros((T, T), f32)
 
-    for cp in small + big:
+    for cp in small:
         cp.wait()
-    live = live_ref[epoch, 0]
-    eye = (lax.broadcasted_iota(i32, (T, T), 0) == lax.broadcasted_iota(i32, (T, T), 1)).astype(bf16)
+    live = live_ref[epoch]
 
     @functools.partial(lax.fori_loop, 0, tiles // 2, init_val=jnp.int32(GROUP))
     def pairs(i, np):
-        for k in range(2):
-            b = i * 2 + k
-            x = uf[rows(b), :].astype(bf16)
-            ub[b] = x
-            utb[b] = lax.dot_general(eye, x, NT, preferred_element_type=f32).astype(bf16)
-            vb[b] = vf[rows(b), :].astype(bf16)
         for k in range(2 * per):
             t = i * (2 * per) + k
             a, b = ut[epoch, t], it[epoch, t]
@@ -81,6 +74,19 @@
             si[b] = si[b] + one
         nb[i] = np
         return np
+
+    for cp in big:
+        cp.wait()
+    eye = (lax.broadcasted_iota(i32, (T, T), 0) == lax.broadcasted_iota(i32, (T, T), 1)).astype(bf16)
+
+    @pl.loop(0, tiles // 4)
+    def _(i):
+        for k in range(4):
+            b = i * 4 + k
+            x = uf[rows(b), :].astype(bf16)
+            ub[b] = x
+            utb[b] = lax.dot_general(eye, x, NT, preferred_element_type=f32).astype(bf16)
+            vb[b] = vf[rows(b), :].astype(bf16)
 
     @functools.partial(lax.fori_loop, 0, tiles, init_val=pairs)
     def total(a, np):
@@ -272,15 +278,15 @@
 
     pend = []
     got1, goty, got2, gote = {}, {}, {}, {}
-    for half in range(2):
-        for c in range(2):
+    for c in range(2):
+        for half in range(2):
             for e in range(2):
                 for d in range(2):
                     i = half * 2 + e
                     yb = hy if half else 1 - hy
                     eb = 1 - h2[d] if e else h2[d]
                     got1[d, c, i] = put(grads.at[tile(d, c, 1 - h1[d], yb, eb)], rx1.at[d, c, i], s1.at[d, c, i], r1.at[d, c, i], first[d])
-        if not half:
+        if not c:
             gotc = [put(counts.at[lax.rem(r + k, n)], cin.at[k - 1], sc.at[k - 1], rc.at[k - 1], (s, lax.rem(r + k, n))) for k in range(1, n)]
     for cp in local:
         cp.wait()
@@ -357,27 +363,28 @@
             send1(d, c, 2 + j, b)
             save(b)
 
-    for c in range(2):
-        take1(c, 0)
-        take1(c, 1)
+    take1(0, 0)
+    take1(0, 1)
+    take1(0, 2)
+    takey(0, 0)
+    take1(0, 3)
     for g in gotc:
         g.wait_recv()
     cmine[...] += functools.reduce(lambda p, q: p + q, [cin[k] for k in range(n - 1)])
-    take1(0, 2)
-    take1(0, 3)
-    takey(0, 0)
     takey(0, 1)
+    take1(1, 0)
+    finish(0)
+    take1(1, 1)
     take1(1, 2)
-    finish(0)
+    takey(1, 0)
     take1(1, 3)
-    takey(1, 0)
     spread(0)
     takey(1, 1)
     finish(1)
     pass2(0)
     passy(0, 0)
+    passy(0, 1)
     spread(1)
-    passy(0, 1)
     pass2(1)
     passy(1, 0)
     passy(1, 1)
@@ -428,6 +435,7 @@
 def local(user_factors, item_factors, ratings, user_tile, item_tile, live_count, partner):
     n = lax.axis_size("replica")
     half = lax.axis_size("stratum") // 2
+    live_count = live_count.reshape(-1)
     users, grads, counts = tiles_step(0, user_tile, item_tile, live_count, user_factors, item_factors, ratings, n)
     branches = [functools.partial(share, mask=half + k, cid=1 + k) for k in range(half)]
     block = lax.switch(partner[0] - half, branches, grads, counts, item_factors)

time: 129 us -> 136 us (1.054)
  Pallas kernels: 123 us -> 131 us
    pallas_call x2, Pallas kernels: 92.5 us -> 98.7 us  [share(): pl.pallas_call(functools.partial(share_kernel, mask), out_shape=(pltpu.HB...]
    pallas_call x2, Pallas kernels: 30.9 us -> 32.7 us  [tiles_step(): pl.pallas_call(functools.partial(tile_kernel, epoch, shards, chunks), out...]
where the time goes in v4:
time: 136 us; the launch traced here: 134 us
  Pallas kernels  131 us (96%)
    pallas_call x2, Pallas kernels, share(): pl.pallas_call(functools.partial(share_kernel, mask), out_shape=(pltpu.HB...  98.7 us
    pallas_call x2, Pallas kernels, tiles_step(): pl.pallas_call(functools.partial(tile_kernel, epoch, shards, chunks), out...  32.7 us

profile of v4, /device:TPU:0, one launch (start us, length us, event | category | flops | bytes accessed | tf_op | source)
XLA Modules:
  0.0 134.4 jit_solution(2843715570345793532)
XLA Ops:
  1.3 16.8 %tile_step_0.1 = (f32[4096,128]{1,0:T(8,128)}, f32[32,128,128]{2,1,0:T(8,128)S(1)}, f32[8,8,128]{2,1,0:T(8,128)S(1)}) custom-call(s32[2,256]{1,0:T(2,128)} %ut_in.3, s32[2,256]{1,0:T(2,128)} %it_in.3, s32[2]{0:T(128)} %bitcast.3, f32[4096,128]{1,0:T(8,128)} %users.1, f32[4096,128]{1,0:T(8,128)} %items.1, bf16[2,256,128,128]{3,2,1,0:T(8,128)(2,1)} %ratings.3), custom_call_target="tpu_custom_call" | custom-call | tf_op jit(solution)/shard_map/tile_step_0/pallas_call | solution.py:199
  18.1 54.4 %conditional.1 = (f32[4096,128]{1,0:T(8,128)}) conditional(s32[]{:T(128)} %bitcast.1, (f32[32,128,128]{2,1,0:T(8,128)S(1)}, f32[8,8,128]{2,1,0:T(8,128)S(1)}, f32[4096,128]{1,0:T(8,128)}) %tuple.32, (f32[32,128,128]{2,1,0:T(8,128)S(1)}, f32[8,8,128]{2,1,0:T(8,128)S(1)}, f32[4096,128]{1,0:T(8,128)}) %tuple.32, ...), branch_computations={%region_0.0_spmd, %region_1.0_spmd, %region_2.0_spmd, %region_3.0_... | conditional | bytes 8 | solution.py:441
  18.1 54.2 %share_10.1 = f32[4096,128]{1,0:T(8,128)} custom-call(f32[32,128,128]{2,1,0:T(8,128)S(1)} %get-tuple-element.59.grads, f32[8,8,128]{2,1,0:T(8,128)S(1)} %get-tuple-element.64.counts, f32[4096,128]{1,0:T(8,128)} %get-tuple-element.65.block), custom_call_target="tpu_custom_call" | custom-call | tf_op jit(solution)/shard_map/cond/branch_2_fun/share_10/pallas_call | solution.py:412
  72.5 0.0 copy-start
  72.5 15.9 %tile_step_1.1 = (f32[4096,128]{1,0:T(8,128)}, f32[32,128,128]{2,1,0:T(8,128)S(1)}, f32[8,8,128]{2,1,0:T(8,128)S(1)}) custom-call(s32[2,256]{1,0:T(2,128)} %ut_in.3, s32[2,256]{1,0:T(2,128)} %it_in.3, s32[2]{0:T(128)} %bitcast.4, f32[4096,128]{1,0:T(8,128)} %get-tuple-element.89.users, f32[4096,128]{1,0:T(8,128)} %get-tuple-element.99.items.block, ...), custom_call_target="tpu_custom_call" | custom-call | tf_op jit(solution)/shard_map/tile_step_1/pallas_call | solution.py:199
  88.5 0.0 copy-done
  88.5 44.5 %share_0.1 = f32[4096,128]{1,0:T(8,128)S(1)} custom-call(f32[32,128,128]{2,1,0:T(8,128)S(1)} %get-tuple-element.93.grads, f32[8,8,128]{2,1,0:T(8,128)S(1)} %get-tuple-element.94.counts, f32[4096,128]{1,0:T(8,128)S(1)} %copy-done), custom_call_target="tpu_custom_call" | custom-call | tf_op jit(solution)/shard_map/share_0/pallas_call | solution.py:412
  133.0 1.3 copy.18
Async XLA Ops:
  72.5 16.0 %copy-start = (f32[4096,128]{1,0:T(8,128)S(1)}, f32[4096,128]{1,0:T(8,128)}, u32[]{:S(2)}) copy-start(f32[4096,128]{1,0:T(8,128)} %get-tuple-element.99.items.block) | copy-start | bytes 6291460

commit v5 on v4

--- a/solution.py
+++ b/solution.py
@@ -41,7 +41,7 @@
     big = [pltpu.make_async_copy(users, uf, msem.at[3]), pltpu.make_async_copy(items, vf, msem.at[4])]
     for cp in small + big:
         cp.start()
-    for c in range(chunks):
+    for c in range(2):
         load(c).start()
 
     @pl.loop(0, tiles)
@@ -75,6 +75,8 @@
         nb[i] = np
         return np
 
+    for c in range(2, chunks):
+        load(c).start()
     for cp in big:
         cp.wait()
     eye = (lax.broadcasted_iota(i32, (T, T), 0) == lax.broadcasted_iota(i32, (T, T), 1)).astype(bf16)
@@ -113,39 +115,35 @@
             out.append((pa[p], x, y, tx, ty, it[epoch, tx], it[epoch, ty]))
         return out
 
-    def flush(g):
-        todo = names(g)
-        gu, gv = [], []
-        for k, (a, x, y, tx, ty, bx, by) in enumerate(todo):
-            r = rbuf[k]
-            v = jnp.concatenate([vb[bx], vb[by]], axis=0)
-            gu.append(lax.dot_general(r, v, NN, preferred_element_type=f32))
-            gv.append(lax.dot_general(utb[a], r, NN, preferred_element_type=f32))
-        return todo, gu, gv
-
-    def fill(g):
-        res = []
-        for k, (a, x, y, tx, ty, bx, by) in enumerate(names(g)):
-            v = jnp.concatenate([vb[bx], vb[by]], axis=0)
-            p = lax.dot_general(ub[a], v, NT, preferred_element_type=f32)
-            r1 = (rat[tx].astype(f32) - p[:, :T]).astype(bf16)
-            r2 = (rat[ty].astype(f32) - p[:, T:]).astype(bf16)
-            zero = jnp.zeros((T, T), bf16)
-            res.append(jnp.concatenate([jnp.where(x >= 0, r1, zero), jnp.where(y >= 0, r2, zero)], axis=1))
-        return res
-
-    def settle(todo, gu, gv):
-        for k, (a, x, y, tx, ty, bx, by) in enumerate(todo):
-            du[a] += gu[k]
-            dv[bx] += gv[k][:, :T]
-            dv[by] += gv[k][:, T:]
+    def flush(k, name):
+        a, x, y, tx, ty, bx, by = name
+        r = rbuf[k]
+        v = jnp.concatenate([vb[bx], vb[by]], axis=0)
+        gu = lax.dot_general(r, v, NN, preferred_element_type=f32)
+        gv = lax.dot_general(utb[a], r, NN, preferred_element_type=f32)
+        return gu, gv
+
+    def settle(name, gu, gv):
+        a, x, y, tx, ty, bx, by = name
+        du[a] += gu
+        dv[bx] += gv[:, :T]
+        dv[by] += gv[:, T:]
+
+    def fill(k, name):
+        a, x, y, tx, ty, bx, by = name
+        v = jnp.concatenate([vb[bx], vb[by]], axis=0)
+        p = lax.dot_general(ub[a], v, NT, preferred_element_type=f32)
+        r1 = (rat[tx].astype(f32) - p[:, :T]).astype(bf16)
+        r2 = (rat[ty].astype(f32) - p[:, T:]).astype(bf16)
+        zero = jnp.zeros((T, T), bf16)
+        rbuf[k] = jnp.concatenate([jnp.where(x >= 0, r1, zero), jnp.where(y >= 0, r2, zero)], axis=1)
 
     def work(g, carry):
-        todo, gu, gv = flush(g)
-        res = fill(g + 1)
+        now, later = names(g), names(g + 1)
         for k in range(GROUP):
-            rbuf[k] = res[k]
-        settle(todo, gu, gv)
+            gu, gv = flush(k, now[k])
+            fill(k, later[k])
+            settle(now[k], gu, gv)
         return carry
 
     def chunk(c, done):
@@ -156,7 +154,9 @@
         return jnp.maximum(done, upto)
 
     ended = lax.fori_loop(0, chunks, chunk, jnp.int32(0))
-    settle(*flush(ended))
+    last = names(ended)
+    for k in range(GROUP):
+        settle(last[k], *flush(k, last[k]))
 
     row = lax.broadcasted_iota(i32, (8, T), 0)
     for r in range(shards):
@@ -278,16 +278,17 @@
 
     pend = []
     got1, goty, got2, gote = {}, {}, {}, {}
-    for c in range(2):
-        for half in range(2):
-            for e in range(2):
-                for d in range(2):
-                    i = half * 2 + e
-                    yb = hy if half else 1 - hy
-                    eb = 1 - h2[d] if e else h2[d]
-                    got1[d, c, i] = put(grads.at[tile(d, c, 1 - h1[d], yb, eb)], rx1.at[d, c, i], s1.at[d, c, i], r1.at[d, c, i], first[d])
-        if not c:
-            gotc = [put(counts.at[lax.rem(r + k, n)], cin.at[k - 1], sc.at[k - 1], rc.at[k - 1], (s, lax.rem(r + k, n))) for k in range(1, n)]
+    def go(c, half):
+        for e in range(2):
+            for d in range(2):
+                i = half * 2 + e
+                yb = hy if half else 1 - hy
+                eb = 1 - h2[d] if e else h2[d]
+                got1[d, c, i] = put(grads.at[tile(d, c, 1 - h1[d], yb, eb)], rx1.at[d, c, i], s1.at[d, c, i], r1.at[d, c, i], first[d])
+
+    go(0, 0)
+    go(0, 1)
+    gotc = [put(counts.at[lax.rem(r + k, n)], cin.at[k - 1], sc.at[k - 1], rc.at[k - 1], (s, lax.rem(r + k, n))) for k in range(1, n)]
     for cp in local:
         cp.wait()
 
@@ -365,27 +366,35 @@
 
     take1(0, 0)
     take1(0, 1)
+    go(1, 0)
     take1(0, 2)
-    takey(0, 0)
     take1(0, 3)
     for g in gotc:
         g.wait_recv()
     cmine[...] += functools.reduce(lambda p, q: p + q, [cin[k] for k in range(n - 1)])
+    takey(0, 0)
+    go(1, 1)
+    take1(1, 0)
+    take1(1, 1)
     takey(0, 1)
-    take1(1, 0)
     finish(0)
-    take1(1, 1)
+    if not mask:
+        spread(0)
     take1(1, 2)
     takey(1, 0)
     take1(1, 3)
-    spread(0)
+    if not mask:
+        pass2(0)
     takey(1, 1)
     finish(1)
-    pass2(0)
+    if mask:
+        spread(0)
+    if mask:
+        pass2(0)
+    spread(1)
     passy(0, 0)
+    pass2(1)
     passy(0, 1)
-    spread(1)
-    pass2(1)
     passy(1, 0)
     passy(1, 1)
     for c in range(2):

time: 136 us -> 122 us (0.90)
  Pallas kernels: 131 us -> 117 us
    pallas_call x2, Pallas kernels: 98.7 us -> 86.7 us  [share(): pl.pallas_call(functools.partial(share_kernel, mask), out_shape=(pltpu.HB...]
    pallas_call x2, Pallas kernels: 32.7 us -> 30.4 us  [tiles_step(): pl.pallas_call(functools.partial(tile_kernel, epoch, shards, chunks), out...]
where the time goes in v5:
time: 122 us; the launch traced here: 120 us
  Pallas kernels  117 us (96%)
  local copies, waits for them, and re-layouts  1.33 us (1%)
  between operations  1.33 us (1%)
    pallas_call x2, Pallas kernels, share(): pl.pallas_call(functools.partial(share_kernel, mask), out_shape=(pltpu.HB...  86.7 us
    pallas_call x2, Pallas kernels, tiles_step(): pl.pallas_call(functools.partial(tile_kernel, epoch, shards, chunks), out...  30.4 us

profile of v5, /device:TPU:0, one launch (start us, length us, event | category | flops | bytes accessed | tf_op | source)
XLA Modules:
  0.0 120.0 jit_solution(11633934387263633753)
XLA Ops:
  1.3 15.6 %tile_step_0.1 = (f32[4096,128]{1,0:T(8,128)}, f32[32,128,128]{2,1,0:T(8,128)S(1)}, f32[8,8,128]{2,1,0:T(8,128)S(1)}) custom-call(s32[2,256]{1,0:T(2,128)} %ut_in.3, s32[2,256]{1,0:T(2,128)} %it_in.3, s32[2]{0:T(128)} %bitcast.3, f32[4096,128]{1,0:T(8,128)} %users.1, f32[4096,128]{1,0:T(8,128)} %items.1, bf16[2,256,128,128]{3,2,1,0:T(8,128)(2,1)} %ratings.3), custom_call_target="tpu_custom_call" | custom-call | tf_op jit(solution)/shard_map/tile_step_0/pallas_call | solution.py:199
  16.9 47.5 %conditional.1 = (f32[4096,128]{1,0:T(8,128)}) conditional(s32[]{:T(128)} %bitcast.1, (f32[32,128,128]{2,1,0:T(8,128)S(1)}, f32[8,8,128]{2,1,0:T(8,128)S(1)}, f32[4096,128]{1,0:T(8,128)}) %tuple.32, (f32[32,128,128]{2,1,0:T(8,128)S(1)}, f32[8,8,128]{2,1,0:T(8,128)S(1)}, f32[4096,128]{1,0:T(8,128)}) %tuple.32, ...), branch_computations={%region_0.0_spmd, %region_1.0_spmd, %region_2.0_spmd, %region_3.0_... | conditional | bytes 8 | solution.py:450
  16.9 47.2 %share_8.1 = f32[4096,128]{1,0:T(8,128)} custom-call(f32[32,128,128]{2,1,0:T(8,128)S(1)} %get-tuple-element.49.grads, f32[8,8,128]{2,1,0:T(8,128)S(1)} %get-tuple-element.50.counts, f32[4096,128]{1,0:T(8,128)} %get-tuple-element.51.block), custom_call_target="tpu_custom_call" | custom-call | tf_op jit(solution)/shard_map/cond/branch_0_fun/share_8/pallas_call | solution.py:421
  64.4 0.0 copy-start
  64.4 14.8 %tile_step_1.1 = (f32[4096,128]{1,0:T(8,128)}, f32[32,128,128]{2,1,0:T(8,128)S(1)}, f32[8,8,128]{2,1,0:T(8,128)S(1)}) custom-call(s32[2,256]{1,0:T(2,128)} %ut_in.3, s32[2,256]{1,0:T(2,128)} %it_in.3, s32[2]{0:T(128)} %bitcast.4, f32[4096,128]{1,0:T(8,128)} %get-tuple-element.89.users, f32[4096,128]{1,0:T(8,128)} %get-tuple-element.99.items.block, ...), custom_call_target="tpu_custom_call" | custom-call | tf_op jit(solution)/shard_map/tile_step_1/pallas_call | solution.py:199
  79.2 0.0 copy-done
  79.2 39.5 %share_0.1 = f32[4096,128]{1,0:T(8,128)S(1)} custom-call(f32[32,128,128]{2,1,0:T(8,128)S(1)} %get-tuple-element.93.grads, f32[8,8,128]{2,1,0:T(8,128)S(1)} %get-tuple-element.94.counts, f32[4096,128]{1,0:T(8,128)S(1)} %copy-done), custom_call_target="tpu_custom_call" | custom-call | tf_op jit(solution)/shard_map/share_0/pallas_call | solution.py:421
  118.7 1.3 %copy.18 = f32[4096,128]{1,0:T(8,128)} copy(f32[4096,128]{1,0:T(8,128)S(1)} %share_0.1) | data formatting | bytes 4194304
Async XLA Ops:
  64.4 14.8 %copy-start = (f32[4096,128]{1,0:T(8,128)S(1)}, f32[4096,128]{1,0:T(8,128)}, u32[]{:S(2)}) copy-start(f32[4096,128]{1,0:T(8,128)} %get-tuple-element.99.items.block) | copy-start | bytes 6291460

commit v6 on v5

--- a/solution.py
+++ b/solution.py
@@ -19,7 +19,7 @@
     return pltpu.with_memory_space_constraint(x, space)
 
 
-def tile_kernel(epoch, shards, chunks, ut_in, it_in, live_in, users, items, ratings,
+def tile_kernel(epoch, chunks, ut_in, it_in, live_in, users, items, ratings,
                 users_out, dv, counts_out,
                 ut, it, live_ref, rat, uf, vf, ub, utb, vb, du,
                 rbuf, pa, p1, p2, nb, pend, su, si, rsem, msem, osem):
@@ -56,8 +56,7 @@
         cp.wait()
     live = live_ref[epoch]
 
-    @functools.partial(lax.fori_loop, 0, tiles // 2, init_val=jnp.int32(GROUP))
-    def pairs(i, np):
+    def pair(i, np):
         for k in range(2 * per):
             t = i * (2 * per) + k
             a, b = ut[epoch, t], it[epoch, t]
@@ -75,20 +74,24 @@
         nb[i] = np
         return np
 
+    early = tiles // 4
+    pairs = lax.fori_loop(0, early, pair, jnp.int32(GROUP))
     for c in range(2, chunks):
         load(c).start()
     for cp in big:
         cp.wait()
     eye = (lax.broadcasted_iota(i32, (T, T), 0) == lax.broadcasted_iota(i32, (T, T), 1)).astype(bf16)
 
-    @pl.loop(0, tiles // 4)
-    def _(i):
+    def cast(i, np):
         for k in range(4):
             b = i * 4 + k
             x = uf[rows(b), :].astype(bf16)
             ub[b] = x
             utb[b] = lax.dot_general(eye, x, NT, preferred_element_type=f32).astype(bf16)
             vb[b] = vf[rows(b), :].astype(bf16)
+        return pair(early + i, np)
+
+    pairs = lax.fori_loop(0, tiles // 4, cast, pairs)
 
     @functools.partial(lax.fori_loop, 0, tiles, init_val=pairs)
     def total(a, np):
@@ -159,16 +162,11 @@
         settle(last[k], *flush(k, last[k]))
 
     row = lax.broadcasted_iota(i32, (8, T), 0)
-    for r in range(shards):
-        x, hy = r // 2, r % 2
-        lo, hi = x % 2, x // 2
+    for h in range(4):
         z = jnp.zeros((8, T), f32)
-        for d in range(2):
-            for c in range(2):
-                b = (d * 2 + c) * 8 + (hi if d else lo ^ hi) * 4 + hy * 2 + lo
-                z = jnp.where(row == d * 2 + c, si[b].astype(f32), z)
-        counts_out[r] = z
-
+        for j in range(8):
+            z = jnp.where(row == j, si[(h // 2 * 2 + j // 4) * 8 + h % 2 * 4 + j % 4].astype(f32), z)
+        counts_out[h] = z
 
     def update(i, carry):
         for k in range(2):
@@ -188,7 +186,7 @@
         cp.wait()
 
 
-def tiles_step(epoch, ut, it, live, users, items, ratings, shards=8, chunks=8):
+def tiles_step(epoch, ut, it, live, users, items, ratings, chunks=8):
     slots, T = ratings.shape[1], ratings.shape[2]
     tiles = users.shape[0] // T
     first = epoch == 0
@@ -197,8 +195,8 @@
     smem = lambda *k: pltpu.SMEM(k, i32)
     length = slots // 2 + tiles + 2 * GROUP
     return pl.pallas_call(
-        functools.partial(tile_kernel, epoch, shards, chunks),
-        out_shape=(pltpu.HBM(users.shape, f32), pltpu.VMEM((tiles, T, T), f32), pltpu.VMEM((shards, 8, T), f32)),
+        functools.partial(tile_kernel, epoch, chunks),
+        out_shape=(pltpu.HBM(users.shape, f32), pltpu.VMEM((tiles, T, T), f32), pltpu.VMEM((4, 8, T), f32)),
         in_specs=[hbm] * 4 + [hbm if first else pl.BlockSpec(memory_space=pl.ANY)] + [hbm],
         out_specs=(hbm, vmem, vmem),
         scratch_shapes=[
@@ -223,7 +221,6 @@
 def share_kernel(mask, grads, counts, block, dest, hold, acc, old, new, rx1, ry, rx2, cin, cmine,
                  s1, r1, sy, ry_s, s2, r2, sc, rc, se, re, t2, q2, ty, qy, t1, q1, lsem, wsem):
     T = block.shape[1]
-    n = counts.shape[0]
     s = lax.axis_index("stratum")
     r = lax.axis_index("replica")
     x, hy = lax.div(r, 2), lax.rem(r, 2)
@@ -257,15 +254,15 @@
             saved[-1].start()
 
     bar = pltpu.get_barrier_semaphore()
-    for k in range(1, n):
-        pl.semaphore_signal(bar, inc=1, device_id=(s, lax.rem(r + k, n)), device_id_type=MESH)
+    for dev in (*first, over):
+        pl.semaphore_signal(bar, inc=1, device_id=dev, device_id_type=MESH)
     across = s
     if mask:
         for bit in range(4):
             if mask >> bit & 1:
                 across = across + (1 << bit) - (2 << bit) * lax.rem(lax.div(s, 1 << bit), 2)
         pl.semaphore_signal(bar, inc=1, device_id=(across, r), device_id_type=MESH)
-    local = [pltpu.make_async_copy(counts.at[r], cmine, lsem.at[1])]
+    local = []
     mine = {}
     for d in range(2):
         for c in range(2):
@@ -274,7 +271,7 @@
             local.append(pltpu.make_async_copy(block.at[rows(b)], old.at[d, c], lsem.at[2 + d * 2 + c]))
     for cp in local:
         cp.start()
-    pl.semaphore_wait(bar, n - 1 + (1 if mask else 0))
+    pl.semaphore_wait(bar, 4 if mask else 3)
 
     pend = []
     got1, goty, got2, gote = {}, {}, {}, {}
@@ -286,9 +283,18 @@
                 eb = 1 - h2[d] if e else h2[d]
                 got1[d, c, i] = put(grads.at[tile(d, c, 1 - h1[d], yb, eb)], rx1.at[d, c, i], s1.at[d, c, i], r1.at[d, c, i], first[d])
 
+    gotc = [put(counts.at[d * 2 + 1 - h1[d]], cin.at[0, d], sc.at[0, d], rc.at[0, d], first[d]) for d in range(2)]
     go(0, 0)
     go(0, 1)
-    gotc = [put(counts.at[lax.rem(r + k, n)], cin.at[k - 1], sc.at[k - 1], rc.at[k - 1], (s, lax.rem(r + k, n))) for k in range(1, n)]
+
+    def tally(step):
+        for d in range(2):
+            gotc[step * 2 + d].wait_recv()
+            before = cmine[step - 1, d] if step else counts[d * 2 + h1[d]]
+            cmine[step, d] = before + cin[step, d]
+            if step < 2:
+                gotc.append(put(cmine.at[step, d], cin.at[step + 1, d], sc.at[step + 1, d], rc.at[step + 1, d], second[d] if step else over))
+
     for cp in local:
         cp.wait()
 
@@ -320,7 +326,7 @@
             b = mine[d, c]
             got2[d, c].wait_recv()
             total = acc[b] + rx2[d, c]
-            cnt = jnp.maximum(cmine[pl.ds(d * 2 + c, 1), :], 1.0)
+            cnt = jnp.maximum(cmine[2, d, pl.ds(c * 4 + hy * 2 + h2[d], 1), :], 1.0)
             fresh = old[d, c] * KEEP + total.T * (LR / cnt)
             if mask:
                 new[d, c] = fresh
@@ -364,19 +370,19 @@
             send1(d, c, 2 + j, b)
             save(b)
 
+    tally(0)
     take1(0, 0)
     take1(0, 1)
     go(1, 0)
     take1(0, 2)
     take1(0, 3)
-    for g in gotc:
-        g.wait_recv()
-    cmine[...] += functools.reduce(lambda p, q: p + q, [cin[k] for k in range(n - 1)])
+    tally(1)
     takey(0, 0)
     go(1, 1)
     take1(1, 0)
     take1(1, 1)
     takey(0, 1)
+    tally(2)
     finish(0)
     if not mask:
         spread(0)
@@ -413,7 +419,6 @@
 
 def share(grads, counts, block, mask, cid):
     tiles, T = grads.shape[0], grads.shape[1]
-    n = counts.shape[0]
     vmem = pl.BlockSpec(memory_space=pltpu.VMEM)
     hbm = pl.BlockSpec(memory_space=pltpu.HBM)
     dma = lambda *k: pltpu.SemaphoreType.DMA(k)
@@ -431,9 +436,9 @@
             pltpu.VMEM((2, 2, 4, T, T), f32),
             pltpu.VMEM((2, 2, 2, T, T), f32),
             pltpu.VMEM((2, 2, T, T), f32),
-            pltpu.VMEM((n - 1, 8, T), f32),
-            pltpu.VMEM((8, T), f32),
-            *both(2, 2, 4), *both(2, 2, 2), *both(2, 2), *both(n - 1), *both(2, 2),
+            pltpu.VMEM((3, 2, 8, T), f32),
+            pltpu.VMEM((3, 2, 8, T), f32),
+            *both(2, 2, 4), *both(2, 2, 2), *both(2, 2), *both(3, 2), *both(2, 2),
             *both(2, 2), *both(2, 2, 2), *both(2, 2, 4), dma(6), dma(tiles),
         ],
         compiler_params=pltpu.CompilerParams(collective_id=cid, has_side_effects=True, vmem_limit_bytes=24 << 20),
@@ -442,13 +447,12 @@
 
 
 def local(user_factors, item_factors, ratings, user_tile, item_tile, live_count, partner):
-    n = lax.axis_size("replica")
     half = lax.axis_size("stratum") // 2
     live_count = live_count.reshape(-1)
-    users, grads, counts = tiles_step(0, user_tile, item_tile, live_count, user_factors, item_factors, ratings, n)
+    users, grads, counts = tiles_step(0, user_tile, item_tile, live_count, user_factors, item_factors, ratings)
     branches = [functools.partial(share, mask=half + k, cid=1 + k) for k in range(half)]
     block = lax.switch(partner[0] - half, branches, grads, counts, item_factors)
-    users, grads, counts = tiles_step(1, user_tile, item_tile, live_count, users, block, ratings, n)
+    users, grads, counts = tiles_step(1, user_tile, item_tile, live_count, users, block, ratings)
     return users, share(grads, counts, block, 0, 0)
 
 

time: 122 us -> 121 us (level); the launches traced: 120 us -> 120 us
  no operation moved by 1% of the time
where the time goes in v6:
time: 121 us; the launch traced here: 120 us
  Pallas kernels  118 us (98%)
  local copies, waits for them, and re-layouts  1.33 us (1%)
  between operations  1.33 us (1%)
    pallas_call x2, Pallas kernels, share(): pl.pallas_call(functools.partial(share_kernel, mask), out_shape=(pltpu.HB...  86.5 us
    pallas_call x2, Pallas kernels, tiles_step(): pl.pallas_call(functools.partial(tile_kernel, epoch, chunks), out_shape=(...  31 us

profile of v6, /device:TPU:0, one launch (start us, length us, event | category | flops | bytes accessed | tf_op | source)
XLA Modules:
  0.0 120.5 jit_solution(18215298969580300836)
XLA Ops:
  1.3 15.0 %tile_step_0.1 = (f32[4096,128]{1,0:T(8,128)}, f32[32,128,128]{2,1,0:T(8,128)S(1)}, f32[4,8,128]{2,1,0:T(8,128)S(1)}) custom-call(s32[2,256]{1,0:T(2,128)} %ut_in.3, s32[2,256]{1,0:T(2,128)} %it_in.3, s32[2]{0:T(128)} %bitcast.3, f32[4096,128]{1,0:T(8,128)} %users.1, f32[4096,128]{1,0:T(8,128)} %items.1, bf16[2,256,128,128]{3,2,1,0:T(8,128)(2,1)} %ratings.3), custom_call_target="tpu_custom_call" | custom-call | tf_op jit(solution)/shard_map/tile_step_0/pallas_call | solution.py:197
  16.3 48.9 %conditional.1 = (f32[4096,128]{1,0:T(8,128)}) conditional(s32[]{:T(128)} %bitcast.1, (f32[32,128,128]{2,1,0:T(8,128)S(1)}, f32[4,8,128]{2,1,0:T(8,128)S(1)}, f32[4096,128]{1,0:T(8,128)}) %tuple.32, (f32[32,128,128]{2,1,0:T(8,128)S(1)}, f32[4,8,128]{2,1,0:T(8,128)S(1)}, f32[4096,128]{1,0:T(8,128)}) %tuple.32, ...), branch_computations={%region_0.0_spmd, %region_1.0_spmd, %region_2.0_spmd, %region_3.0_... | conditional | bytes 8 | solution.py:454
  16.3 48.6 %share_11.1 = f32[4096,128]{1,0:T(8,128)} custom-call(f32[32,128,128]{2,1,0:T(8,128)S(1)} %get-tuple-element.66.grads, f32[4,8,128]{2,1,0:T(8,128)S(1)} %get-tuple-element.67.counts, f32[4096,128]{1,0:T(8,128)} %get-tuple-element.68.block), custom_call_target="tpu_custom_call" | custom-call | tf_op jit(solution)/shard_map/cond/branch_3_fun/share_11/pallas_call | solution.py:426
  65.2 0.0 copy-start
  65.2 16.0 %tile_step_1.1 = (f32[4096,128]{1,0:T(8,128)}, f32[32,128,128]{2,1,0:T(8,128)S(1)}, f32[4,8,128]{2,1,0:T(8,128)S(1)}) custom-call(s32[2,256]{1,0:T(2,128)} %ut_in.3, s32[2,256]{1,0:T(2,128)} %it_in.3, s32[2]{0:T(128)} %bitcast.4, f32[4096,128]{1,0:T(8,128)} %get-tuple-element.89.users, f32[4096,128]{1,0:T(8,128)} %get-tuple-element.99.items.block, ...), custom_call_target="tpu_custom_call" | custom-call | tf_op jit(solution)/shard_map/tile_step_1/pallas_call | solution.py:197
  81.2 0.0 copy-done
  81.3 37.9 %share_0.1 = f32[4096,128]{1,0:T(8,128)S(1)} custom-call(f32[32,128,128]{2,1,0:T(8,128)S(1)} %get-tuple-element.93.grads, f32[4,8,128]{2,1,0:T(8,128)S(1)} %get-tuple-element.94.counts, f32[4096,128]{1,0:T(8,128)S(1)} %copy-done), custom_call_target="tpu_custom_call" | custom-call | tf_op jit(solution)/shard_map/share_0/pallas_call | solution.py:426
  119.1 1.3 %copy.18 = f32[4096,128]{1,0:T(8,128)} copy(f32[4096,128]{1,0:T(8,128)S(1)} %share_0.1) | data formatting | bytes 4194304
Async XLA Ops:
  65.2 16.0 %copy-start = (f32[4096,128]{1,0:T(8,128)S(1)}, f32[4096,128]{1,0:T(8,128)}, u32[]{:S(2)}) copy-start(f32[4096,128]{1,0:T(8,128)} %get-tuple-element.99.items.block) | copy-start | bytes 6291460

commit v7 on v6

--- a/solution.py
+++ b/solution.py
@@ -20,13 +20,15 @@
 
 
 def tile_kernel(epoch, chunks, ut_in, it_in, live_in, users, items, ratings,
-                users_out, dv, counts_out,
+                users_out, dv, counts_out, seen_out,
                 ut, it, live_ref, rat, uf, vf, ub, utb, vb, du,
                 rbuf, pa, p1, p2, nb, pend, su, si, rsem, msem, osem):
     tiles, T = ub.shape[0], ub.shape[1]
     slots = rat.shape[0]
     width = slots // chunks
     first = epoch == 0
+    if first:
+        du = users_out
     per = slots // tiles
 
     def load(c):
@@ -168,6 +170,15 @@
             z = jnp.where(row == j, si[(h // 2 * 2 + j // 4) * 8 + h % 2 * 4 + j % 4].astype(f32), z)
         counts_out[h] = z
 
+    if first:
+        for h in range(tiles // 8):
+            z = jnp.zeros((8, T), f32)
+            for j in range(8):
+                z = jnp.where(row == j, jnp.maximum(su[h * 8 + j], 1).astype(f32), z)
+            seen_out[pl.ds(h * 8, 8), :] = z
+        return
+    seen_out[...] = jnp.zeros(seen_out.shape, f32)
+
     def update(i, carry):
         for k in range(2):
             b = i * 2 + k
@@ -196,16 +207,16 @@
     length = slots // 2 + tiles + 2 * GROUP
     return pl.pallas_call(
         functools.partial(tile_kernel, epoch, chunks),
-        out_shape=(pltpu.HBM(users.shape, f32), pltpu.VMEM((tiles, T, T), f32), pltpu.VMEM((4, 8, T), f32)),
+        out_shape=(pltpu.VMEM((tiles, T, T), f32) if first else pltpu.HBM(users.shape, f32), pltpu.VMEM((tiles, T, T), f32), pltpu.VMEM((4, 8, T), f32), pltpu.VMEM((tiles, T), f32)),
         in_specs=[hbm] * 4 + [hbm if first else pl.BlockSpec(memory_space=pl.ANY)] + [hbm],
-        out_specs=(hbm, vmem, vmem),
+        out_specs=(vmem if first else hbm, vmem, vmem, vmem),
         scratch_shapes=[
             smem(*ut.shape), smem(*it.shape), smem(*live.shape),
             pltpu.VMEM((slots, T, T), bf16),
             pltpu.VMEM(users.shape, f32),
             pltpu.VMEM(items.shape, f32),
             pltpu.VMEM((tiles, T, T), bf16), pltpu.VMEM((tiles, T, T), bf16), pltpu.VMEM((tiles, T, T), bf16),
-            pltpu.VMEM((tiles, T, T), f32),
+            pltpu.VMEM((8, T) if first else (tiles, T, T), f32),
             pltpu.VMEM((GROUP, T, 2 * T), bf16),
             smem(length), smem(length), smem(length), smem(tiles // 2), smem(tiles), smem(tiles), smem(tiles),
             pltpu.SemaphoreType.DMA((chunks,)), pltpu.SemaphoreType.DMA((5,)), pltpu.SemaphoreType.DMA((4,)),
@@ -218,7 +229,15 @@
 MESH = pl.DeviceIdType.MESH
 
 
-def share_kernel(mask, grads, counts, block, dest, hold, acc, old, new, rx1, ry, rx2, cin, cmine,
+def share_kernel(mask, grads, counts, block, *rest):
+    if mask:
+        users, user_grad, seen, dest, users_out, *rest, ubuf, usem, osem = rest
+    else:
+        dest, *rest = rest
+    share_body(mask, grads, counts, block, dest, (users, user_grad, seen, users_out, ubuf, usem, osem) if mask else None, *rest)
+
+
+def share_body(mask, grads, counts, block, dest, extra, hold, acc, old, new, rx1, ry, rx2, cin, cmine,
                  s1, r1, sy, ry_s, s2, r2, sc, rc, se, re, t2, q2, ty, qy, t1, q1, lsem, wsem):
     T = block.shape[1]
     s = lax.axis_index("stratum")
@@ -263,6 +282,25 @@
                 across = across + (1 << bit) - (2 << bit) * lax.rem(lax.div(s, 1 << bit), 2)
         pl.semaphore_signal(bar, inc=1, device_id=(across, r), device_id_type=MESH)
     local = []
+    parts = []
+    if mask:
+        users, user_grad, seen, users_out, ubuf, usem, osem = extra
+        fetch = pltpu.make_async_copy(users, ubuf, usem)
+        fetch.start()
+    quarter = grads.shape[0] // 4
+
+    def improve(part):
+        if not mask:
+            return
+
+        @pl.loop(part * quarter, (part + 1) * quarter)
+        def _(b):
+            ubuf[rows(b), :] = ubuf[rows(b), :] * KEEP + user_grad[b] * (LR / seen[pl.ds(b, 1), :])
+
+        o = pl.ds(part * quarter * T, quarter * T)
+        parts.append(pltpu.make_async_copy(ubuf.at[o], users_out.at[o], osem.at[part]))
+        parts[-1].start()
+
     mine = {}
     for d in range(2):
         for c in range(2):
@@ -387,20 +425,26 @@
     if not mask:
         spread(0)
     take1(1, 2)
+    if mask:
+        fetch.wait()
+    improve(0)
     takey(1, 0)
     take1(1, 3)
     if not mask:
         pass2(0)
     takey(1, 1)
     finish(1)
+    improve(1)
     if mask:
         spread(0)
     if mask:
         pass2(0)
     spread(1)
     passy(0, 0)
+    improve(2)
     pass2(1)
     passy(0, 1)
+    improve(3)
     passy(1, 0)
     passy(1, 1)
     for c in range(2):
@@ -413,11 +457,11 @@
             cp.wait_send()
     for g in gotc:
         g.wait_send()
-    for cp in saved:
+    for cp in saved + parts:
         cp.wait()
 
 
-def share(grads, counts, block, mask, cid):
+def share(grads, counts, block, *more, mask, cid):
     tiles, T = grads.shape[0], grads.shape[1]
     vmem = pl.BlockSpec(memory_space=pltpu.VMEM)
     hbm = pl.BlockSpec(memory_space=pltpu.HBM)
@@ -425,9 +469,9 @@
     both = lambda *k: [dma(*k), dma(*k)]
     return pl.pallas_call(
         functools.partial(share_kernel, mask),
-        out_shape=(pltpu.HBM if mask else pltpu.VMEM)(block.shape, f32),
-        in_specs=[vmem, vmem, hbm if mask else pl.BlockSpec(memory_space=pl.ANY)],
-        out_specs=hbm if mask else vmem,
+        out_shape=(pltpu.HBM(block.shape, f32),) * 2 if mask else pltpu.VMEM(block.shape, f32),
+        in_specs=[vmem, vmem, hbm if mask else pl.BlockSpec(memory_space=pl.ANY)] + ([hbm, vmem, vmem] if mask else []),
+        out_specs=(hbm, hbm) if mask else vmem,
         scratch_shapes=[
             pltpu.VMEM(block.shape if mask else (8, T), f32),
             pltpu.VMEM((tiles, T, T), f32),
@@ -440,20 +484,21 @@
             pltpu.VMEM((3, 2, 8, T), f32),
             *both(2, 2, 4), *both(2, 2, 2), *both(2, 2), *both(3, 2), *both(2, 2),
             *both(2, 2), *both(2, 2, 2), *both(2, 2, 4), dma(6), dma(tiles),
+            *([pltpu.VMEM(block.shape, f32), pltpu.SemaphoreType.DMA, dma(4)] if mask else []),
         ],
         compiler_params=pltpu.CompilerParams(collective_id=cid, has_side_effects=True, vmem_limit_bytes=24 << 20),
         name=f"share_{mask}",
-    )(grads, counts, pin(block) if mask else block)
+    )(grads, counts, pin(block) if mask else block, *((pin(more[0]), *more[1:]) if mask else ()))
 
 
 def local(user_factors, item_factors, ratings, user_tile, item_tile, live_count, partner):
     half = lax.axis_size("stratum") // 2
     live_count = live_count.reshape(-1)
-    users, grads, counts = tiles_step(0, user_tile, item_tile, live_count, user_factors, item_factors, ratings)
+    user_grad, grads, counts, seen = tiles_step(0, user_tile, item_tile, live_count, user_factors, item_factors, ratings)
     branches = [functools.partial(share, mask=half + k, cid=1 + k) for k in range(half)]
-    block = lax.switch(partner[0] - half, branches, grads, counts, item_factors)
-    users, grads, counts = tiles_step(1, user_tile, item_tile, live_count, users, block, ratings)
-    return users, share(grads, counts, block, 0, 0)
+    block, users = lax.switch(partner[0] - half, branches, grads, counts, item_factors, user_factors, user_grad, seen)
+    users, grads, counts, _ = tiles_step(1, user_tile, item_tile, live_count, users, block, ratings)
+    return users, share(grads, counts, block, mask=0, cid=0)
 
 
 def solution(mesh):

time: 121 us -> 116 us (0.959)
  Pallas kernels: 118 us -> 113 us
    pallas_call x2, Pallas kernels: 31 us -> 28.3 us  [tiles_step(): pl.pallas_call(functools.partial(tile_kernel, epoch, chunks), out_shape=(...]
    pallas_call x2, Pallas kernels: 86.5 us -> 85.1 us  [share(): pl.pallas_call(functools.partial(share_kernel, mask), out_shape=(pltpu.HB...]
where the time goes in v7:
time: 116 us
  Pallas kernels  113 us (97%)
  local copies, waits for them, and re-layouts  1.33 us (1%)
  between operations  1.33 us (1%)
    pallas_call x2, Pallas kernels, share(): pl.pallas_call(functools.partial(share_kernel, mask), out_shape=(pltpu.HB...  85.1 us
    pallas_call x2, Pallas kernels, tiles_step(): pl.pallas_call(functools.partial(tile_kernel, epoch, chunks), out_shape=(...  28.3 us

profile of v7, /device:TPU:0, one launch (start us, length us, event | category | flops | bytes accessed | tf_op | source)
XLA Modules:
  0.0 116.3 jit_solution(14179406320208345529)
XLA Ops:
  1.3 11.6 %tile_step_0.1 = (f32[32,128,128]{2,1,0:T(8,128)S(1)}, f32[32,128,128]{2,1,0:T(8,128)S(1)}, f32[4,8,128]{2,1,0:T(8,128)S(1)}, f32[32,128]{1,0:T(8,128)S(1)}) custom-call(s32[2,256]{1,0:T(2,128)} %ut_in.3, s32[2,256]{1,0:T(2,128)} %it_in.3, s32[2]{0:T(128)} %bitcast.3, f32[4096,128]{1,0:T(8,128)} %users.1, f32[4096,128]{1,0:T(8,128)} %items.1, ...), custom_call_target="tpu_custom_call" | custom-call | tf_op jit(solution)/shard_map/tile_step_0/pallas_call | solution.py:208
  12.9 49.4 %conditional.1 = ((f32[4096,128]{1,0:T(8,128)}, f32[4096,128]{1,0:T(8,128)})) conditional(s32[]{:T(128)} %bitcast.1, (f32[32,128,128]{2,1,0:T(8,128)S(1)}, f32[4,8,128]{2,1,0:T(8,128)S(1)}, f32[4096,128]{1,0:T(8,128)}, f32[4096,128]{1,0:T(8,128)}, f32[32,128,128]{2,1,0:T(8,128)S(1)}, ...), branch_computations={%region_0.0_spmd, %region_1.0_spmd, %region_2.0_spmd, %region_3.0_... | conditional | bytes 8 | solution.py:499
  13.0 49.2 %share_11.1 = (f32[4096,128]{1,0:T(8,128)}, f32[4096,128]{1,0:T(8,128)}) custom-call(f32[32,128,128]{2,1,0:T(8,128)S(1)} %get-tuple-element.114.grads, f32[4,8,128]{2,1,0:T(8,128)S(1)} %get-tuple-element.115.counts, f32[4096,128]{1,0:T(8,128)} %get-tuple-element.116.block, f32[4096,128]{1,0:T(8,128)} %get-tuple-element.117.rest_0_, ...), custom_call_target="tpu_custom_call" | custom-call | tf_op jit(solution)/shard_map/cond/branch_3_fun/share_11/pallas_call | solution.py:470
  62.4 0.0 copy-start
  62.4 16.6 %tile_step_1.1 = (f32[4096,128]{1,0:T(8,128)}, f32[32,128,128]{2,1,0:T(8,128)S(1)}, f32[4,8,128]{2,1,0:T(8,128)S(1)}, f32[32,128]{1,0:T(8,128)}) custom-call(s32[2,256]{1,0:T(2,128)} %ut_in.3, s32[2,256]{1,0:T(2,128)} %it_in.3, s32[2]{0:T(128)} %bitcast.4, f32[4096,128]{1,0:T(8,128)} %get-tuple-element.159.users, ...), custom_call_target="tpu_custom_call" | custom-call | tf_op jit(solution)/shard_map/tile_step_1/pallas_call | solution.py:208
  79.0 0.0 copy-done
  79.0 35.9 %share_0.1 = f32[4096,128]{1,0:T(8,128)S(1)} custom-call(f32[32,128,128]{2,1,0:T(8,128)S(1)} %get-tuple-element.162.grads, f32[4,8,128]{2,1,0:T(8,128)S(1)} %get-tuple-element.163.counts, f32[4096,128]{1,0:T(8,128)S(1)} %copy-done), custom_call_target="tpu_custom_call" | custom-call | tf_op jit(solution)/shard_map/share_0/pallas_call | solution.py:470
  114.9 1.3 %copy.26 = f32[4096,128]{1,0:T(8,128)} copy(f32[4096,128]{1,0:T(8,128)S(1)} %share_0.1) | data formatting | bytes 4194304
Async XLA Ops:
  62.4 16.6 %copy-start = (f32[4096,128]{1,0:T(8,128)S(1)}, f32[4096,128]{1,0:T(8,128)}, u32[]{:S(2)}) copy-start(f32[4096,128]{1,0:T(8,128)} %get-tuple-element.160.items.block) | copy-start | bytes 6291460

commit v8 on v7

--- a/solution.py
+++ b/solution.py
@@ -12,7 +12,7 @@
 NT = (((1,), (1,)), ((), ()))
 NN = (((1,), (0,)), ((), ()))
 f32, bf16, i32 = jnp.float32, jnp.bfloat16, jnp.int32
-GROUP = 16
+GROUP = 20
 
 
 def pin(x, space=pltpu.HBM):
@@ -432,10 +432,12 @@
     take1(1, 3)
     if not mask:
         pass2(0)
+    if mask and not mask & 2:
+        spread(0)
     takey(1, 1)
     finish(1)
     improve(1)
-    if mask:
+    if mask & 2:
         spread(0)
     if mask:
         pass2(0)

time: 116 us -> 114 us (0.983); the launches traced: 116 us -> 112 us
  Pallas kernels: 113 us -> 109 us
    pallas_call x2, Pallas kernels: 28.3 us -> 23.2 us  [tiles_step(): pl.pallas_call(functools.partial(tile_kernel, epoch, chunks), out_shape=(...]
where the time goes in v8:
time: 114 us; the launch traced here: 112 us
  Pallas kernels  109 us (96%)
  local copies, waits for them, and re-layouts  1.33 us (1%)
  between operations  1.33 us (1%)
    pallas_call x2, Pallas kernels, share(): pl.pallas_call(functools.partial(share_kernel, mask), out_shape=(pltpu.HB...  85.5 us
    pallas_call x2, Pallas kernels, tiles_step(): pl.pallas_call(functools.partial(tile_kernel, epoch, chunks), out_shape=(...  23.2 us

profile of v8, /device:TPU:0, one launch (start us, length us, event | category | flops | bytes accessed | tf_op | source)
XLA Modules:
  0.0 111.6 jit_solution(4624634192187645869)
XLA Ops:
  1.3 10.7 %tile_step_0.1 = (f32[32,128,128]{2,1,0:T(8,128)S(1)}, f32[32,128,128]{2,1,0:T(8,128)S(1)}, f32[4,8,128]{2,1,0:T(8,128)S(1)}, f32[32,128]{1,0:T(8,128)S(1)}) custom-call(s32[2,256]{1,0:T(2,128)} %ut_in.3, s32[2,256]{1,0:T(2,128)} %it_in.3, s32[2]{0:T(128)} %bitcast.3, f32[4096,128]{1,0:T(8,128)} %users.1, f32[4096,128]{1,0:T(8,128)} %items.1, ...), custom_call_target="tpu_custom_call" | custom-call | tf_op jit(solution)/shard_map/tile_step_0/pallas_call | solution.py:208
  12.0 48.2 %conditional.1 = ((f32[4096,128]{1,0:T(8,128)}, f32[4096,128]{1,0:T(8,128)})) conditional(s32[]{:T(128)} %bitcast.1, (f32[32,128,128]{2,1,0:T(8,128)S(1)}, f32[4,8,128]{2,1,0:T(8,128)S(1)}, f32[4096,128]{1,0:T(8,128)}, f32[4096,128]{1,0:T(8,128)}, f32[32,128,128]{2,1,0:T(8,128)S(1)}, ...), branch_computations={%region_0.0_spmd, %region_1.0_spmd, %region_2.0_spmd, %region_3.0_... | conditional | bytes 8 | solution.py:501
  12.0 48.0 %share_12.1 = (f32[4096,128]{1,0:T(8,128)}, f32[4096,128]{1,0:T(8,128)}) custom-call(f32[32,128,128]{2,1,0:T(8,128)S(1)} %get-tuple-element.120.grads, f32[4,8,128]{2,1,0:T(8,128)S(1)} %get-tuple-element.121.counts, f32[4096,128]{1,0:T(8,128)} %get-tuple-element.122.block, f32[4096,128]{1,0:T(8,128)} %get-tuple-element.123.rest_0_, ...), custom_call_target="tpu_custom_call" | custom-call | tf_op jit(solution)/shard_map/cond/branch_4_fun/share_12/pallas_call | solution.py:472
  60.2 0.0 copy-start
  60.2 12.5 %tile_step_1.1 = (f32[4096,128]{1,0:T(8,128)}, f32[32,128,128]{2,1,0:T(8,128)S(1)}, f32[4,8,128]{2,1,0:T(8,128)S(1)}, f32[32,128]{1,0:T(8,128)}) custom-call(s32[2,256]{1,0:T(2,128)} %ut_in.3, s32[2,256]{1,0:T(2,128)} %it_in.3, s32[2]{0:T(128)} %bitcast.4, f32[4096,128]{1,0:T(8,128)} %get-tuple-element.159.users, ...), custom_call_target="tpu_custom_call" | custom-call | tf_op jit(solution)/shard_map/tile_step_1/pallas_call | solution.py:208
  72.8 0.0 copy-done
  72.8 37.5 %share_0.1 = f32[4096,128]{1,0:T(8,128)S(1)} custom-call(f32[32,128,128]{2,1,0:T(8,128)S(1)} %get-tuple-element.162.grads, f32[4,8,128]{2,1,0:T(8,128)S(1)} %get-tuple-element.163.counts, f32[4096,128]{1,0:T(8,128)S(1)} %copy-done), custom_call_target="tpu_custom_call" | custom-call | tf_op jit(solution)/shard_map/share_0/pallas_call | solution.py:472
  110.3 1.3 %copy.26 = f32[4096,128]{1,0:T(8,128)} copy(f32[4096,128]{1,0:T(8,128)S(1)} %share_0.1) | data formatting | bytes 4194304
Async XLA Ops:
  60.2 12.6 %copy-start = (f32[4096,128]{1,0:T(8,128)S(1)}, f32[4096,128]{1,0:T(8,128)}, u32[]{:S(2)}) copy-start(f32[4096,128]{1,0:T(8,128)} %get-tuple-element.160.items.block) | copy-start | bytes 6291460
